TPU v7x, 32 devices: a whole 2x2x4 slice. The times are simulated.
32 devices in a mesh: groups: 2 (over x), tile: 16 (over z, y, core).
Axes of the slice: x: 2, y: 2, z: 4, core: 2. Of those that a mesh axis runs over, the one named last changes fastest.
Arguments:
- walkers: bfloat16 [32, 512, 256], P(('groups', 'tile')), parts along dimension 0, may hold values from -6 to 6
- green_factor: bfloat16 [32, 512, 256], P(('groups', 'tile')), parts along dimension 0, may hold values from -6 to 6
- trial: bfloat16 [512, 256], replicated, may hold values from -0.375 to 0.375
- chol: bfloat16 [496, 2048, 256], P('tile'), may hold values from -0.01171875 to 0.01171875
- pattern: int32 [256], replicated, may hold values from 0 to 1023, as said below
- owner_counts: int32 [16], replicated, may hold values from 1 to 31, as said below
- chol_group: int32 [2048], replicated, may hold values from 0 to 3
- group_weight: float32 [4], replicated, may hold values from 0.5 to 2
- aux: int32 [32, 2048], P('groups'), parts along dimension 0, may hold values from -524288 to 524287
Outputs:
- advanced: bfloat16 [32, 512, 256], P(('groups', 'tile')), parts along dimension 0
- log_weight: float32 [32], P(('groups', 'tile')), parts along dimension 0
There are 2 independent parts, one for each index of `groups`. A program takes and returns all parts, laid end to end along the dimension named above; an argument that names none is the same for every part. Nothing has to cross between parts.
Inputs may be any that keep to these rules, and one draw needn't show every extreme that they name: `pattern`: values are distinct. Owners d and d + 8 together hold 32 tiles; slots of owner d past owner_counts[d] hold no tile.
All inputs are finite; a program needn't handle non-finite values.
Results may differ from a plain program's by a relative error of at most 0.009.
Values may be sent and summed in bfloat16 or wider, within the bound.
No kernel may reach another device: no remote copies, remote signals or barrier semaphores. Data moves between devices by JAX's collectives and lax.ppermute only.
A program may use at most 128 MiB of HBM per device.

v0:
```python
import functools
import math

import jax
import jax.numpy as jnp
from jax import lax
from jax.experimental import pallas as pl
from jax.experimental.pallas import tpu as pltpu
from jax.sharding import PartitionSpec as P

BF = jnp.bfloat16
F32 = jnp.float32
LANES = 128
VMEM_LIMIT = 60 * 1024 * 1024


def log2(n):
    bits = n.bit_length() - 1
    assert 1 << bits == n
    return bits


def iota(shape, axis):
    return lax.broadcasted_iota(jnp.int32, shape, axis)


def one_hot(equal):
    return jnp.where(equal, 1.0, 0.0).astype(BF)


def mm(a, b):
    return jnp.dot(a, b, preferred_element_type=F32)


def nt(a, b):
    return lax.dot_general(a, b, (((1,), (1,)), ((), ())), preferred_element_type=F32)


def swap_rows(outer, inner):
    n = outer * inner
    row, col = iota((n, n), 0), iota((n, n), 1)
    source = ((row & (outer - 1)) << log2(inner)) + (row >> log2(outer))
    return one_hot(source == col)


def regroup(x, outer, inner, chunk):
    take = swap_rows(chunk, inner)
    size = chunk * inner
    parts = [mm(take, x[i * size : (i + 1) * size]).astype(BF) for i in range(outer // chunk)]
    if len(parts) == 1:
        return parts[0]
    return jnp.concatenate(
        [part[b * chunk : (b + 1) * chunk] for b in range(inner) for part in parts], axis=0
    )


def ungroup(x, outer, inner, chunk):
    take = swap_rows(inner, chunk)
    parts = []
    for i in range(outer // chunk):
        rows = [x[b * outer + i * chunk : b * outer + (i + 1) * chunk] for b in range(inner)]
        piece = x if outer == chunk else jnp.concatenate(rows, axis=0)
        parts.append(mm(take, piece).astype(BF))
    return parts[0] if len(parts) == 1 else jnp.concatenate(parts, axis=0)


def slot_of_tile(counts_ref, tiles, owners, groups, half, cap):
    tile = iota((1, tiles), 1)
    owner = jnp.zeros((1, tiles), jnp.int32)
    first = jnp.zeros((1, tiles), jnp.int32)
    offset = jnp.int32(0)
    for d in range(owners):
        offset = offset + counts_ref[d]
        past = tile >= offset
        owner = jnp.where(past, d + 1, owner)
        first = jnp.where(past, offset, first)
    place = tile - first
    slot = owner * half + place
    for x in range(1, groups):
        start = min(x * half, cap - half)
        slot = jnp.where(place >= x * half, (x * owners + owner) * half + place - start, slot)
    return slot


def tile_columns(pattern_ref, tiles, nblk, side):
    pat = jnp.broadcast_to(pattern_ref[...].astype(F32), (LANES, tiles)).T.astype(jnp.int32)
    row_block = pat >> log2(nblk)
    col_block = pat & (nblk - 1)
    per = LANES // side
    return ((col_block >> log2(per)) << log2(nblk)) + row_block, col_block & (per - 1)


def green_kernel(
    counts_ref, pattern_ref, factor_ref, trial_ref, out_ref, *, owners, groups, half, cap, side
):
    orbitals = factor_ref.shape[0]
    nblk = orbitals // side
    tiles = pattern_ref.shape[1]
    wide = orbitals // LANES
    factor = mm(swap_rows(nblk, side), factor_ref[...]).astype(BF)
    green = nt(factor, trial_ref[...]).astype(BF)
    cut = jnp.concatenate(
        [
            jnp.concatenate(
                [
                    green[p * nblk : (p + 1) * nblk, k * LANES : (k + 1) * LANES]
                    for p in range(side)
                ],
                axis=1,
            )
            for k in range(wide)
        ],
        axis=0,
    )
    where_row, place = tile_columns(pattern_ref, tiles, nblk, side)
    lane = iota((tiles, LANES), 1)
    pick = one_hot(where_row == lane)
    inside = place == (lane >> log2(side))
    found = mm(pick, cut)
    kept = jnp.concatenate(
        [
            jnp.where(inside, found[:, p * LANES : (p + 1) * LANES], 0.0).astype(BF)
            for p in range(side)
        ],
        axis=1,
    )
    entries = side * side
    src = iota((side * LANES, entries), 0)
    dst = iota((side * LANES, entries), 1)
    fold = one_hot(((src >> log2(LANES)) << log2(side)) + (src & (side - 1)) == dst)
    values = mm(kept, fold).astype(BF)
    slot = slot_of_tile(counts_ref, tiles, owners, groups, half, cap)
    slots = out_ref.shape[0]
    out_ref[...] = mm(one_hot(iota((slots, tiles), 0) == slot), values).astype(BF)


def start_tiles(start_ref, chol_ref, held, sems, half):
    def begin(j, carry):
        pltpu.make_async_copy(chol_ref.at[start_ref[0] + j], held.at[j], sems.at[j]).start()
        return carry

    lax.fori_loop(0, half, begin, 0)


def wait_tile(chol_ref, held, sems, j):
    pltpu.make_async_copy(chol_ref.at[0], held.at[j], sems.at[j]).wait()


def bias_kernel(start_ref, green_ref, chol_ref, out_ref, held, rows, total, sems, *, walkers, half):
    start_tiles(start_ref, chol_ref, held, sems, half)
    chunk = min(walkers, max(1, 512 // half))
    rows[...] = regroup(green_ref[...], walkers, half, chunk)
    total[...] = jnp.zeros_like(total)

    def step(j, carry):
        wait_tile(chol_ref, held, sems, j)
        left = rows[pl.ds(pl.multiple_of(j * walkers, walkers), walkers), :]
        total[...] += nt(left, held[j])
        return carry

    lax.fori_loop(0, half, step, 0)
    vectors = total.shape[1]
    lanes = vectors // LANES
    stacked = jnp.concatenate(
        [total[:, i * LANES : (i + 1) * LANES].astype(BF) for i in range(lanes)], axis=0
    )
    out_ref[...] = ungroup(stacked, walkers, lanes, min(walkers, max(1, 512 // lanes)))


def field_kernel(
    index_ref, weight_ref, partial_ref, aux_ref, group_ref, fields_ref, logw_ref, *, devices
):
    lanes = group_ref.shape[0]
    bias = jnp.zeros((lanes, LANES), F32)
    for i in range(devices):
        bias = bias + partial_ref[i].astype(F32)
    draws = aux_ref[pl.ds(index_ref[0], 1), :]
    draws = jnp.concatenate(
        [draws[:, i * LANES : (i + 1) * LANES] for i in range(lanes)], axis=0
    )
    sampled = draws.astype(F32) * (1.0 / 262144.0)
    weight = jnp.zeros((lanes, LANES), F32)
    for k in range(weight_ref.shape[0]):
        weight = jnp.where(group_ref[...] == k, weight_ref[k], weight)
    fields = (weight * (sampled - bias)).astype(BF)
    for i in range(devices):
        fields_ref[i] = fields
    logw_ref[0] = jnp.sum(sampled * bias - 0.5 * bias * bias)


def potential_kernel(start_ref, fields_ref, chol_ref, out_ref, held, left, rows, sems, *, walkers, half):
    start_tiles(start_ref, chol_ref, held, sems, half)
    vectors = left.shape[1]
    lanes = vectors // LANES
    stacked = regroup(fields_ref[...], walkers, lanes, min(walkers, max(1, 512 // lanes)))
    for i in range(lanes):
        left[:, i * LANES : (i + 1) * LANES] = stacked[i * walkers : (i + 1) * walkers]

    def step(j, carry):
        wait_tile(chol_ref, held, sems, j)
        rows[pl.ds(pl.multiple_of(j * walkers, walkers), walkers), :] = mm(
            left[...], held[j]
        ).astype(BF)
        return carry

    lax.fori_loop(0, half, step, 0)
    out_ref[...] = ungroup(rows[...], walkers, half, min(walkers, max(1, 512 // half)))


def advance_kernel(
    counts_ref, pattern_ref, tiles_ref, walker_ref, out_ref, *, owners, groups, half, cap, side
):
    orbitals = walker_ref.shape[0]
    nblk = orbitals // side
    tiles = pattern_ref.shape[1]
    wide = orbitals // LANES
    entries = side * side
    slots = tiles_ref.shape[0]
    slot = slot_of_tile(counts_ref, tiles, owners, groups, half, cap)
    place_in = one_hot(iota((slots, tiles), 0) == slot)
    values = lax.dot_general(
        place_in, tiles_ref[...], (((0,), (0,)), ((), ())), preferred_element_type=F32
    ).astype(BF)
    src = iota((entries, side * LANES), 0)
    dst = iota((entries, side * LANES), 1)
    spread = one_hot(((dst >> log2(LANES)) << log2(side)) + (dst & (side - 1)) == src)
    where_row, place = tile_columns(pattern_ref, tiles, nblk, side)
    lane = iota((tiles, LANES), 1)
    inside = place == (lane >> log2(side))
    repeated = mm(values, spread)
    kept = jnp.concatenate(
        [
            jnp.where(inside, repeated[:, p * LANES : (p + 1) * LANES], 0.0).astype(BF)
            for p in range(side)
        ],
        axis=1,
    )
    pick = one_hot(where_row == lane)
    cut = lax.dot_general(
        pick, kept, (((0,), (0,)), ((), ())), preferred_element_type=F32
    ).astype(BF)
    mixed = jnp.concatenate(
        [
            jnp.concatenate(
                [
                    cut[k * nblk : (k + 1) * nblk, p * LANES : (p + 1) * LANES]
                    for k in range(wide)
                ],
                axis=1,
            )
            for p in range(side)
        ],
        axis=0,
    )
    potential = mm(swap_rows(side, nblk), mixed).astype(BF)
    term = walker_ref[...]
    running = term.astype(F32)
    for degree in range(1, 5):
        term = (mm(potential, term) / degree).astype(BF)
        running = running + term.astype(F32)
    out_ref[...] = running.astype(BF)


def per_device(
    walkers, green_factor, trial, chol, pattern, owner_counts, chol_group, group_weight, aux, *, groups, owners
):
    devices = groups * owners
    walk_dev, orbitals, electrons = walkers.shape
    assert walk_dev == 1
    cap, vectors, entries = chol.shape
    side = math.isqrt(entries)
    lanes = vectors // LANES
    half = -(-cap // groups)
    tiles = pattern.shape[0]
    both = ("groups", "tile")
    my_group = lax.axis_index("groups")
    start = jnp.minimum(my_group * half, cap - half).astype(jnp.int32).reshape(1)
    my_index = lax.axis_index("tile").astype(jnp.int32).reshape(1)
    pattern_row = pattern.reshape(1, tiles)

    smem = pl.BlockSpec(memory_space=pltpu.SMEM)
    vmem = pl.BlockSpec(memory_space=pltpu.VMEM)
    hbm = pl.BlockSpec(memory_space=pl.ANY)
    params = pltpu.CompilerParams(vmem_limit_bytes=VMEM_LIMIT)
    sizes = dict(owners=owners, groups=groups, half=half, cap=cap, side=side)

    outgoing = pl.pallas_call(
        functools.partial(green_kernel, **sizes),
        out_shape=jax.ShapeDtypeStruct((devices * half, entries), BF),
        in_specs=[smem, vmem, vmem, vmem],
        out_specs=vmem,
        compiler_params=params,
        name="green",
    )(owner_counts, pattern_row, green_factor[0], trial)
    arrived = lax.all_to_all(
        outgoing.reshape(devices, half, entries), both, split_axis=0, concat_axis=0
    )
    partial_bias = pl.pallas_call(
        functools.partial(bias_kernel, walkers=devices, half=half),
        out_shape=jax.ShapeDtypeStruct((devices * lanes, LANES), BF),
        in_specs=[smem, vmem, hbm],
        out_specs=vmem,
        scratch_shapes=[
            pltpu.VMEM((half, vectors, entries), BF),
            pltpu.VMEM((half * devices, entries), BF),
            pltpu.VMEM((devices, vectors), F32),
            pltpu.SemaphoreType.DMA((half,)),
        ],
        compiler_params=params,
        name="bias",
    )(start, arrived.reshape(devices * half, entries), chol)
    partial_bias = lax.all_to_all(
        partial_bias.reshape(devices, lanes, LANES), both, split_axis=0, concat_axis=0
    )
    fields, log_weight = pl.pallas_call(
        functools.partial(field_kernel, devices=devices),
        out_shape=(
            jax.ShapeDtypeStruct((devices, lanes, LANES), BF),
            jax.ShapeDtypeStruct((1,), F32),
        ),
        in_specs=[smem, smem, vmem, vmem, vmem],
        out_specs=(vmem, smem),
        compiler_params=params,
        name="fields",
    )(my_index, group_weight, partial_bias, aux, chol_group.reshape(lanes, LANES))
    fields = lax.all_to_all(fields, both, split_axis=0, concat_axis=0)
    potential = pl.pallas_call(
        functools.partial(potential_kernel, walkers=devices, half=half),
        out_shape=jax.ShapeDtypeStruct((devices * half, entries), BF),
        in_specs=[smem, vmem, hbm],
        out_specs=vmem,
        scratch_shapes=[
            pltpu.VMEM((half, vectors, entries), BF),
            pltpu.VMEM((devices, vectors), BF),
            pltpu.VMEM((half * devices, entries), BF),
            pltpu.SemaphoreType.DMA((half,)),
        ],
        compiler_params=params,
        name="potential",
    )(start, fields.reshape(devices * lanes, LANES), chol)
    returned = lax.all_to_all(
        potential.reshape(devices, half, entries), both, split_axis=0, concat_axis=0
    )
    advanced = pl.pallas_call(
        functools.partial(advance_kernel, **sizes),
        out_shape=jax.ShapeDtypeStruct((orbitals, electrons), BF),
        in_specs=[smem, vmem, vmem, vmem],
        out_specs=vmem,
        compiler_params=params,
        name="advance",
    )(owner_counts, pattern_row, returned.reshape(devices * half, entries), walkers[0])
    return advanced[None], log_weight


def solution(mesh):
    return jax.shard_map(
        functools.partial(
            per_device, groups=mesh.shape["groups"], owners=mesh.shape["tile"]
        ),
        mesh=mesh,
        in_specs=(
            P(("groups", "tile"), None, None),
            P(("groups", "tile"), None, None),
            P(),
            P("tile", None, None),
            P(),
            P(),
            P(),
            P(),
            P("groups", None),
        ),
        out_specs=(P(("groups", "tile"), None, None), P(("groups", "tile"))),
        check_vma=False,
    )
```

profile of v0, /device:TPU:0, one launch (start us, length us, event | category | flops | bytes accessed | tf_op | source)
XLA Modules:
  0.0 83.0 jit_solution(8347326905080088090)
XLA Ops:
  0.6 3.5 %green.1 = bf16[512,256]{1,0:T(8,128)(2,1)} custom-call(s32[16]{0:T(128)} %counts_ref.3, s32[1,256]{1,0:T(1,128)} %bitcast.23, bf16[512,256]{1,0:T(8,128)(2,1)} %bitcast.19, bf16[512,256]{1,0:T(8,128)(2,1)} %trial_ref.1), custom_call_target="tpu_custom_call" | custom-call | tf_op jit(solution)/shard_map/green/pallas_call | solution.py:287
  4.1 7.3 %all-to-all-start = ((bf16[32,16,256]{2,1,0:T(8,128)(2,1)}), bf16[32,16,256]{2,1,0:T(8,128)(2,1)S(1)}, u32[]{:S(2)}, u32[]{:S(2)}) async-start(bf16[32,16,256]{2,1,0:T(8,128)(2,1)} %bitcast.15), calls=%async_computation | async-start | bytes 524288 | tf_op jit(solution)/shard_map/all_to_all | solution.py:295
  11.4 10.2 %all-to-all-done = bf16[32,16,256]{2,1,0:T(8,128)(2,1)S(1)} async-done(((bf16[32,16,256]{2,1,0:T(8,128)(2,1)}), bf16[32,16,256]{2,1,0:T(8,128)(2,1)S(1)}, u32[]{:S(2)}, u32[]{:S(2)}) %all-to-all-start) | async-done | bytes 262176 | tf_op jit(solution)/shard_map/all_to_all | solution.py:295
  21.7 0.0 copy-start
  21.7 0.7 copy-done
  22.4 10.0 %bias.1 = bf16[512,128]{1,0:T(8,128)(2,1)} custom-call(s32[1]{0:T(128)} %bitcast.1.start_ref, bf16[512,256]{1,0:T(8,128)(2,1)} %bitcast.13, bf16[31,2048,256]{2,1,0:T(8,128)(2,1)} %chol_ref.3), custom_call_target="tpu_custom_call" | custom-call | tf_op jit(solution)/shard_map/bias/pallas_call | solution.py:298
  32.4 2.6 %all-to-all-start.1 = ((bf16[32,16,128]{2,1,0:T(8,128)(2,1)}), bf16[32,16,128]{2,1,0:T(8,128)(2,1)S(1)}, u32[]{:S(2)}, u32[]{:S(2)}) async-start(bf16[32,16,128]{2,1,0:T(8,128)(2,1)} %bitcast.17), calls=%async_computation.1 | async-start | bytes 262144 | tf_op jit(solution)/shard_map/all_to_all | solution.py:312
  35.0 8.2 %all-to-all-done.1.partial_ref = bf16[32,16,128]{2,1,0:T(8,128)(2,1)S(1)} async-done(((bf16[32,16,128]{2,1,0:T(8,128)(2,1)}), bf16[32,16,128]{2,1,0:T(8,128)(2,1)S(1)}, u32[]{:S(2)}, u32[]{:S(2)}) %all-to-all-start.1) | async-done | bytes 131104 | tf_op jit(solution)/shard_map/all_to_all | solution.py:312
  43.2 0.0 copy-start.1
  43.2 0.7 copy-done.1
  43.8 1.7 %fields.1 = (bf16[32,16,128]{2,1,0:T(8,128)(2,1)}, f32[1]{0:T(128)}) custom-call(s32[1]{0:T(128)} %bitcast.2.index_ref, f32[4]{0:T(128)} %weight_ref.1, bf16[32,16,128]{2,1,0:T(8,128)(2,1)} %copy-done.1, s32[16,2048]{1,0:T(8,128)} %aux_ref.1, s32[16,128]{1,0:T(8,128)} %bitcast.22), custom_call_target="tpu_custom_call" | custom-call | tf_op jit(solution)/shard_map/fields/pallas_call | solution.py:315
  45.5 11.5 %all_to_all.20 = bf16[32,16,128]{2,1,0:T(8,128)(2,1)} all-to-all(bf16[32,16,128]{2,1,0:T(8,128)(2,1)} %get-tuple-element.4), channel_id=1, replica_groups=mesh['groups'=2,'tile'=16] {'groups','tile'}, dimensions={0} | all-to-all | bytes 262144 | tf_op jit(solution)/shard_map/all_to_all | solution.py:326
  57.0 8.1 %potential.1 = bf16[512,256]{1,0:T(8,128)(2,1)} custom-call(s32[1]{0:T(128)} %bitcast.1.start_ref, bf16[512,128]{1,0:T(8,128)(2,1)} %bitcast.18, bf16[31,2048,256]{2,1,0:T(8,128)(2,1)} %chol_ref.3), custom_call_target="tpu_custom_call" | custom-call | tf_op jit(solution)/shard_map/potential/pallas_call | solution.py:327
  65.1 13.6 %all_to_all.21 = bf16[32,16,256]{2,1,0:T(8,128)(2,1)} all-to-all(bf16[32,16,256]{2,1,0:T(8,128)(2,1)} %bitcast.14), channel_id=1, replica_groups=mesh['groups'=2,'tile'=16] {'groups','tile'}, dimensions={0} | all-to-all | bytes 524288 | tf_op jit(solution)/shard_map/all_to_all | solution.py:341
  78.7 4.3 %advance.1 = bf16[512,256]{1,0:T(8,128)(2,1)} custom-call(s32[16]{0:T(128)} %counts_ref.3, s32[1,256]{1,0:T(1,128)} %bitcast.24, bf16[512,256]{1,0:T(8,128)(2,1)} %bitcast.16, bf16[512,256]{1,0:T(8,128)(2,1)} %bitcast.20), custom_call_target="tpu_custom_call" | custom-call | tf_op jit(solution)/shard_map/advance/pallas_call | solution.py:344
Async XLA Ops:
  4.1 17.6 %all-to-all-start = ((bf16[32,16,256]{2,1,0:T(8,128)(2,1)}), bf16[32,16,256]{2,1,0:T(8,128)(2,1)S(1)}, u32[]{:S(2)}, u32[]{:S(2)}) async-start(bf16[32,16,256]{2,1,0:T(8,128)(2,1)} %bitcast.15), calls=%async_computation | async-start | bytes 524288 | tf_op jit(solution)/shard_map/all_to_all | solution.py:295
  21.7 0.7 copy-start
  32.4 10.8 %all-to-all-start.1 = ((bf16[32,16,128]{2,1,0:T(8,128)(2,1)}), bf16[32,16,128]{2,1,0:T(8,128)(2,1)S(1)}, u32[]{:S(2)}, u32[]{:S(2)}) async-start(bf16[32,16,128]{2,1,0:T(8,128)(2,1)} %bitcast.17), calls=%async_computation.1 | async-start | bytes 262144 | tf_op jit(solution)/shard_map/all_to_all | solution.py:312
  43.2 0.7 copy-start.1
where the time goes:
time: 83.4 us; the launch traced here: 83 us
  Pallas kernels  27.6 us (33%)
  blocking collectives  25 us (30%)
  waiting for transfers between devices  18.4 us (22%)
  starting transfers between devices  9.91 us (12%)
  local copies, waits for them, and re-layouts  1.36 us (2%)
    all_to_all x1, blocking collectives, per_device(): lax.all_to_all(potential.reshape(devices, half, entries), both, split_axi...  13.6 us
    all_to_all x1, blocking collectives, per_device(): fields = lax.all_to_all(fields, both, split_axis=0, concat_axis=0)  11.5 us
    all_to_all x1, waiting for transfers between devices, per_device(): lax.all_to_all(outgoing.reshape(devices, half, entries), both, split_axis...  10.2 us
    pallas_call x1, Pallas kernels, per_device(): pl.pallas_call(functools.partial(bias_kernel, walkers=devices, half=half)...  9.97 us
    all_to_all x1, waiting for transfers between devices, per_device(): lax.all_to_all(partial_bias.reshape(devices, lanes, LANES), both, split_a...  8.2 us
    pallas_call x1, Pallas kernels, per_device(): pl.pallas_call(functools.partial(potential_kernel, walkers=devices, half=...  8.12 us
    all_to_all x1, starting transfers between devices, per_device(): lax.all_to_all(outgoing.reshape(devices, half, entries), both, split_axis...  7.32 us
    pallas_call x1, Pallas kernels, per_device(): pl.pallas_call(functools.partial(advance_kernel, **sizes), out_shape=jax....  4.31 us
  transfers between devices with their start and end apart: 2, of which 2 were waited for; matrix products, arithmetic and copies ran while one was open for 0% of the time, Pallas kernels for 0%

commit v1 on v0

v1 whole, which is shorter than its diff:
```python
import functools
import math

import jax
import jax.numpy as jnp
from jax import lax
from jax.experimental import pallas as pl
from jax.experimental.pallas import tpu as pltpu
from jax.sharding import PartitionSpec as P

BF = jnp.bfloat16
F32 = jnp.float32
LANES = 128
VMEM_LIMIT = 8 * 1024 * 1024


def log2(n):
    bits = n.bit_length() - 1
    assert 1 << bits == n
    return bits


def iota(shape, axis):
    return lax.broadcasted_iota(jnp.int32, shape, axis)


def one_hot(equal):
    return jnp.where(equal, 1.0, 0.0).astype(BF)


def mm(a, b):
    return jnp.dot(a, b, preferred_element_type=F32)


def nt(a, b):
    return lax.dot_general(a, b, (((1,), (1,)), ((), ())), preferred_element_type=F32)


def slot_of_tile(counts_ref, tiles, owners, groups, half, cap):
    tile = iota((1, tiles), 1)
    owner = jnp.zeros((1, tiles), jnp.int32)
    first = jnp.zeros((1, tiles), jnp.int32)
    offset = jnp.int32(0)
    for d in range(owners):
        offset = offset + counts_ref[d]
        past = tile >= offset
        owner = jnp.where(past, d + 1, owner)
        first = jnp.where(past, offset, first)
    place = tile - first
    slot = owner * half + place
    for x in range(1, groups):
        start = min(x * half, cap - half)
        slot = jnp.where(place >= x * half, (x * owners + owner) * half + place - start, slot)
    return slot


def tile_columns(pattern_ref, tiles, nblk, side):
    pat = jnp.broadcast_to(pattern_ref[...].astype(F32), (LANES, tiles)).T.astype(jnp.int32)
    row_block = pat >> log2(nblk)
    col_block = pat & (nblk - 1)
    per = LANES // side
    return ((col_block >> log2(per)) << log2(nblk)) + row_block, col_block & (per - 1)


def green_kernel(
    counts_ref, pattern_ref, factor_ref, trial_ref, out_ref, wide_ref, *, owners, groups, half, cap, side
):
    orbitals = factor_ref.shape[0]
    nblk = orbitals // side
    tiles = pattern_ref.shape[1]
    wide = orbitals // LANES
    assert wide * nblk == LANES
    green = nt(factor_ref[...], trial_ref[...])
    for k in range(wide):
        wide_ref[k] = green[:, k * LANES : (k + 1) * LANES]
    cut = jnp.concatenate(
        [
            jnp.concatenate(
                [wide_ref[k, pl.ds(p, nblk, stride=side), :] for p in range(side)], axis=1
            ).astype(BF)
            for k in range(wide)
        ],
        axis=0,
    )
    where_row, place = tile_columns(pattern_ref, tiles, nblk, side)
    lane = iota((tiles, LANES), 1)
    pick = one_hot(where_row == lane)
    inside = place == (lane >> log2(side))
    found = mm(pick, cut)
    kept = jnp.concatenate(
        [
            jnp.where(inside, found[:, p * LANES : (p + 1) * LANES], 0.0).astype(BF)
            for p in range(side)
        ],
        axis=1,
    )
    entries = side * side
    src = iota((side * LANES, entries), 0)
    dst = iota((side * LANES, entries), 1)
    fold = one_hot(((src >> log2(LANES)) << log2(side)) + (src & (side - 1)) == dst)
    values = mm(kept, fold).astype(BF)
    slot = slot_of_tile(counts_ref, tiles, owners, groups, half, cap)
    slots = out_ref.shape[0]
    out_ref[...] = mm(one_hot(iota((slots, tiles), 0) == slot), values).astype(BF)


def first_slot(half, cap):
    return jnp.minimum(lax.axis_index("groups") * half, cap - half)


def block_sizes(vectors):
    if vectors % 1024:
        return [vectors]
    return [512] * (vectors // 512 - 1) + [256, 256]


def bias_kernel(green_ref, chol_ref, out_ref, tall, left, back, held, sems, *, walkers, half):
    entries = green_ref.shape[1]
    vectors = held.shape[1]
    lanes = vectors // LANES
    narrow = entries // LANES
    first = first_slot(half, chol_ref.shape[0])
    blocks = block_sizes(vectors)
    starts = [sum(blocks[:s]) for s in range(len(blocks))]
    part = half // 4 if half % 4 == 0 else 1
    copies = [
        [
            pltpu.make_async_copy(
                chol_ref.at[pl.ds(first + j, part), pl.ds(at, size), :],
                held.at[pl.ds(j, part), pl.ds(at, size), :],
                sems.at[s, j // part],
            )
            for j in range(0, half, part)
        ]
        for s, (at, size) in enumerate(zip(starts, blocks))
    ]
    for group in copies:
        for copy in group:
            copy.start()
    for k in range(narrow):
        tall[k] = green_ref[:, k * LANES : (k + 1) * LANES].astype(F32)
    for j in range(half):
        for k in range(narrow):
            at = j * entries + k * LANES
            left[:, at : at + LANES] = tall[k, pl.ds(j, walkers, stride=half), :].astype(BF)
    for at, size, group in zip(starts, blocks, copies):
        for copy in group:
            copy.wait()
        right = jnp.concatenate([held[j, at : at + size, :] for j in range(half)], axis=1)
        total = nt(left[...], right)
        for i in range(size // LANES):
            back[pl.ds(at // LANES + i, walkers, stride=lanes), :] = total[
                :, i * LANES : (i + 1) * LANES
            ]
    out_ref[...] = back[...].astype(BF)


def field_kernel(
    weight_ref, partial_ref, aux_ref, group_ref, fields_ref, logw_ref, *, devices
):
    lanes = group_ref.shape[0]
    bias = jnp.zeros((lanes, LANES), F32)
    for i in range(devices):
        bias = bias + partial_ref[i].astype(F32)
    draws = aux_ref[pl.ds(lax.axis_index("tile"), 1), :]
    draws = jnp.concatenate(
        [draws[:, i * LANES : (i + 1) * LANES] for i in range(lanes)], axis=0
    )
    sampled = draws.astype(F32) * (1.0 / 262144.0)
    weight = jnp.zeros((lanes, LANES), F32)
    for k in range(weight_ref.shape[0]):
        weight = jnp.where(group_ref[...] == k, weight_ref[k], weight)
    fields = (weight * (sampled - bias)).astype(BF)
    for i in range(devices):
        fields_ref[i] = fields
    logw_ref[0] = jnp.sum(sampled * bias - 0.5 * bias * bias)


def potential_kernel(fields_ref, chol_ref, out_ref, tall, left, back, held, sems, *, walkers, half):
    entries = held.shape[2]
    lanes = left.shape[1] // LANES
    narrow = entries // LANES
    first = first_slot(half, chol_ref.shape[0])
    copies = [
        pltpu.make_async_copy(chol_ref.at[first + j], held.at[j], sems.at[j]) for j in range(half)
    ]
    for copy in copies:
        copy.start()
    tall[...] = fields_ref[...].astype(F32)
    for i in range(lanes):
        left[:, i * LANES : (i + 1) * LANES] = tall[pl.ds(i, walkers, stride=lanes), :].astype(BF)
    for j in range(half):
        copies[j].wait()
        tile = mm(left[...], held[j])
        for k in range(narrow):
            back[k, pl.ds(j, walkers, stride=half), :] = tile[:, k * LANES : (k + 1) * LANES]
    for k in range(narrow):
        out_ref[:, k * LANES : (k + 1) * LANES] = back[k].astype(BF)


def advance_kernel(
    counts_ref, pattern_ref, tiles_ref, walker_ref, out_ref, wide_ref, *, owners, groups, half, cap, side
):
    orbitals = walker_ref.shape[0]
    nblk = orbitals // side
    tiles = pattern_ref.shape[1]
    wide = orbitals // LANES
    entries = side * side
    slots = tiles_ref.shape[0]
    slot = slot_of_tile(counts_ref, tiles, owners, groups, half, cap)
    place_in = one_hot(iota((slots, tiles), 0) == slot)
    values = lax.dot_general(
        place_in, tiles_ref[...], (((0,), (0,)), ((), ())), preferred_element_type=F32
    ).astype(BF)
    src = iota((entries, side * LANES), 0)
    dst = iota((entries, side * LANES), 1)
    spread = one_hot(((dst >> log2(LANES)) << log2(side)) + (dst & (side - 1)) == src)
    where_row, place = tile_columns(pattern_ref, tiles, nblk, side)
    lane = iota((tiles, LANES), 1)
    inside = place == (lane >> log2(side))
    repeated = mm(values, spread)
    kept = jnp.concatenate(
        [
            jnp.where(inside, repeated[:, p * LANES : (p + 1) * LANES], 0.0).astype(BF)
            for p in range(side)
        ],
        axis=1,
    )
    pick = one_hot(where_row == lane)
    cut = lax.dot_general(
        pick, kept, (((0,), (0,)), ((), ())), preferred_element_type=F32
    )
    for k in range(wide):
        for p in range(side):
            wide_ref[k, pl.ds(p, nblk, stride=side), :] = cut[
                k * nblk : (k + 1) * nblk, p * LANES : (p + 1) * LANES
            ]
    potential = jnp.concatenate([wide_ref[k].astype(BF) for k in range(wide)], axis=1)
    term = walker_ref[...]
    running = term.astype(F32)
    for degree in range(1, 5):
        term = (mm(potential, term) / degree).astype(BF)
        running = running + term.astype(F32)
    out_ref[...] = running.astype(BF)


def per_device(
    walkers, green_factor, trial, chol, pattern, owner_counts, chol_group, group_weight, aux, *, groups, owners
):
    devices = groups * owners
    walk_dev, orbitals, electrons = walkers.shape
    assert walk_dev == 1
    cap, vectors, entries = chol.shape
    side = math.isqrt(entries)
    lanes = vectors // LANES
    half = -(-cap // groups)
    tiles = pattern.shape[0]
    both = ("groups", "tile")
    pattern_row = pattern.reshape(1, tiles)

    smem = pl.BlockSpec(memory_space=pltpu.SMEM)
    vmem = pl.BlockSpec(memory_space=pltpu.VMEM)
    params = pltpu.CompilerParams(vmem_limit_bytes=VMEM_LIMIT)
    hbm = pl.BlockSpec(memory_space=pl.ANY)
    streaming = pltpu.CompilerParams(
        vmem_limit_bytes=VMEM_LIMIT + 2 * half * vectors * entries
    )
    large = pltpu.CompilerParams(vmem_limit_bytes=60 * 1024 * 1024)
    sizes = dict(owners=owners, groups=groups, half=half, cap=cap, side=side)
    tile_bytes = half * vectors * entries * 2
    flops = 2 * devices * half * vectors * entries
    wide_scratch = pltpu.VMEM((orbitals // LANES, orbitals, LANES), F32)

    outgoing = pl.pallas_call(
        functools.partial(green_kernel, **sizes),
        out_shape=jax.ShapeDtypeStruct((devices * half, entries), BF),
        in_specs=[smem, vmem, vmem, vmem],
        out_specs=vmem,
        scratch_shapes=[wide_scratch],
        compiler_params=large,
        name="green",
    )(owner_counts, pattern_row, green_factor[0], trial)
    arrived = lax.all_to_all(
        outgoing.reshape(devices, half, entries), both, split_axis=0, concat_axis=0
    )
    partial_bias = pl.pallas_call(
        functools.partial(bias_kernel, walkers=devices, half=half),
        out_shape=jax.ShapeDtypeStruct((devices * lanes, LANES), BF),
        in_specs=[vmem, hbm],
        out_specs=vmem,
        scratch_shapes=[
            pltpu.VMEM((entries // LANES, half * devices, LANES), F32),
            pltpu.VMEM((devices, half * entries), BF),
            pltpu.VMEM((devices * lanes, LANES), F32),
            pltpu.VMEM((half, vectors, entries), BF),
            pltpu.SemaphoreType.DMA((len(block_sizes(vectors)), half)),
        ],
        compiler_params=streaming,
        cost_estimate=pl.CostEstimate(
            flops=flops, transcendentals=0, bytes_accessed=tile_bytes
        ),
        name="bias",
    )(arrived.reshape(devices * half, entries), chol)
    partial_bias = lax.all_to_all(
        partial_bias.reshape(devices, lanes, LANES), both, split_axis=0, concat_axis=0
    )
    fields, log_weight = pl.pallas_call(
        functools.partial(field_kernel, devices=devices),
        out_shape=(
            jax.ShapeDtypeStruct((devices, lanes, LANES), BF),
            jax.ShapeDtypeStruct((1,), F32),
        ),
        in_specs=[smem, vmem, vmem, vmem],
        out_specs=(vmem, smem),
        compiler_params=params,
        name="fields",
    )(group_weight, partial_bias, aux, chol_group.reshape(lanes, LANES))
    fields = lax.all_to_all(fields, both, split_axis=0, concat_axis=0)
    potential = pl.pallas_call(
        functools.partial(potential_kernel, walkers=devices, half=half),
        out_shape=jax.ShapeDtypeStruct((devices * half, entries), BF),
        in_specs=[vmem, hbm],
        out_specs=vmem,
        scratch_shapes=[
            pltpu.VMEM((devices * lanes, LANES), F32),
            pltpu.VMEM((devices, vectors), BF),
            pltpu.VMEM((entries // LANES, half * devices, LANES), F32),
            pltpu.VMEM((half, vectors, entries), BF),
            pltpu.SemaphoreType.DMA((half,)),
        ],
        compiler_params=streaming,
        cost_estimate=pl.CostEstimate(
            flops=flops, transcendentals=0, bytes_accessed=tile_bytes
        ),
        name="potential",
    )(fields.reshape(devices * lanes, LANES), chol)
    returned = lax.all_to_all(
        potential.reshape(devices, half, entries), both, split_axis=0, concat_axis=0
    )
    advanced = pl.pallas_call(
        functools.partial(advance_kernel, **sizes),
        out_shape=jax.ShapeDtypeStruct((orbitals, electrons), BF),
        in_specs=[smem, vmem, vmem, vmem],
        out_specs=vmem,
        scratch_shapes=[wide_scratch],
        compiler_params=params,
        name="advance",
    )(owner_counts, pattern_row, returned.reshape(devices * half, entries), walkers[0])
    return advanced[None], log_weight


def solution(mesh):
    return jax.shard_map(
        functools.partial(
            per_device, groups=mesh.shape["groups"], owners=mesh.shape["tile"]
        ),
        mesh=mesh,
        in_specs=(
            P(("groups", "tile"), None, None),
            P(("groups", "tile"), None, None),
            P(),
            P("tile", None, None),
            P(),
            P(),
            P(),
            P(),
            P("groups", None),
        ),
        out_specs=(P(("groups", "tile"), None, None), P(("groups", "tile"))),
        check_vma=False,
    )
```

time: 83.4 us -> 76.6 us (0.918)
  blocking collectives: 25 us -> 50 us
  waiting for transfers between devices: 18.4 us -> 0 us
  starting transfers between devices: 9.91 us -> 0 us
  Pallas kernels: 27.6 us -> 25.6 us
  local copies, waits for them, and re-layouts: 1.36 us -> 0.02 us
    all_to_all x0 -> x2, blocking collectives: none -> 28.1 us  [the longest x1 17.6 us: per_device(): lax.all_to_all(outgoing.reshape(devices, half, entries), both, split_axis...]
    all_to_all x2 -> x0, waiting for transfers between devices: 18.4 us -> none  [the longest x1 10.2 us: per_device(): lax.all_to_all(outgoing.reshape(devices, half, entries), both, split_axis...]
    all_to_all x2 -> x0, starting transfers between devices: 9.91 us -> none  [the longest x1 7.32 us: per_device(): lax.all_to_all(outgoing.reshape(devices, half, entries), both, split_axis...]
    all_to_all x1, blocking collectives: 13.6 us -> 12 us  [per_device(): lax.all_to_all(potential.reshape(devices, half, entries), both, split_axi...]
    all_to_all x1, blocking collectives: 11.5 us -> 9.91 us  [per_device(): fields = lax.all_to_all(fields, both, split_axis=0, concat_axis=0)]
    unnamed x4 -> x12, local copies, waits for them, and re-layouts: 1.36 us -> 0.02 us
  transfers between devices with their start and end apart: 2 -> 0, of which waited for: 2 -> 0; matrix products, arithmetic and copies ran while one was open for 0% -> 0% of each run, Pallas kernels for 0% -> 0%
where the time goes in v1:
time: 76.6 us; the launch traced here: 76.3 us
  blocking collectives  50 us (65%)
  Pallas kernels  25.6 us (33%)
    all_to_all x1, blocking collectives, per_device(): lax.all_to_all(outgoing.reshape(devices, half, entries), both, split_axis...  17.6 us
    all_to_all x1, blocking collectives, per_device(): lax.all_to_all(potential.reshape(devices, half, entries), both, split_axi...  12 us
    all_to_all x1, blocking collectives, per_device(): lax.all_to_all(partial_bias.reshape(devices, lanes, LANES), both, split_a...  10.5 us
    all_to_all x1, blocking collectives, per_device(): fields = lax.all_to_all(fields, both, split_axis=0, concat_axis=0)  9.91 us
    pallas_call x1, Pallas kernels, per_device(): pl.pallas_call(functools.partial(bias_kernel, walkers=devices, half=half)...  9.38 us
    pallas_call x1, Pallas kernels, per_device(): pl.pallas_call(functools.partial(potential_kernel, walkers=devices, half=...  7.78 us
    pallas_call x1, Pallas kernels, per_device(): pl.pallas_call(functools.partial(advance_kernel, **sizes), out_shape=jax....  3.7 us
    pallas_call x1, Pallas kernels, per_device(): pl.pallas_call(functools.partial(green_kernel, **sizes), out_shape=jax.Sh...  3.55 us

profile of v1, /device:TPU:0, one launch (start us, length us, event | category | flops | bytes accessed | tf_op | source)
XLA Modules:
  0.0 76.3 jit_solution(5487576255598335460)
XLA Ops:
  0.6 0.0 copy-start.1
  0.6 0.0 copy-start.5
  0.7 0.0 copy-start.2
  0.7 3.6 %green.1 = bf16[512,256]{1,0:T(8,128)(2,1)} custom-call(s32[16]{0:T(128)} %counts_ref.3, s32[1,256]{1,0:T(1,128)} %bitcast.18, bf16[512,256]{1,0:T(8,128)(2,1)} %bitcast.21, bf16[512,256]{1,0:T(8,128)(2,1)} %trial_ref.1), custom_call_target="tpu_custom_call" | custom-call | tf_op jit(solution)/shard_map/green/pallas_call | solution.py:274
  4.2 17.6 %all_to_all.20 = bf16[32,16,256]{2,1,0:T(8,128)(2,1)S(1)} all-to-all(bf16[32,16,256]{2,1,0:T(8,128)(2,1)} %bitcast.20), channel_id=1, replica_groups=mesh['groups'=2,'tile'=16] {'groups','tile'}, dimensions={0} | all-to-all | bytes 524288 | tf_op jit(solution)/shard_map/all_to_all | solution.py:283
  21.8 0.0 copy-start
  21.8 0.0 copy-start.3
  21.8 0.0 copy-start.4
  21.8 9.4 %bias.1 = bf16[512,128]{1,0:T(8,128)(2,1)S(1)} custom-call(bf16[512,256]{1,0:T(8,128)(2,1)S(1)} %bitcast.11, bf16[31,2048,256]{2,1,0:T(8,128)(2,1)} %chol_ref.3), custom_call_target="tpu_custom_call" | custom-call | flops 536870912 | bytes 16777216 | tf_op jit(solution)/shard_map/bias/pallas_call | solution.py:286
  31.2 10.5 %all_to_all.21.partial_ref = bf16[32,16,128]{2,1,0:T(8,128)(2,1)S(1)} all-to-all(bf16[32,16,128]{2,1,0:T(8,128)(2,1)S(1)} %bitcast.14), channel_id=1, replica_groups=mesh['groups'=2,'tile'=16] {'groups','tile'}, dimensions={0} | all-to-all | bytes 262144 | tf_op jit(solution)/shard_map/all_to_all | solution.py:304
  41.7 0.0 copy-done.1
  41.7 0.0 copy-done.5
  41.7 0.0 copy-done.2
  41.7 1.2 %fields.1 = (bf16[32,16,128]{2,1,0:T(8,128)(2,1)S(1)}, f32[1]{0:T(128)}) custom-call(f32[4]{0:T(128)S(1)} %copy-done.5, bf16[32,16,128]{2,1,0:T(8,128)(2,1)S(1)} %all_to_all.21.partial_ref, s32[16,2048]{1,0:T(8,128)S(1)} %copy-done.1, s32[16,128]{1,0:T(8,128)S(1)} %bitcast.17), custom_call_target="tpu_custom_call" | custom-call | tf_op jit(solution)/shard_map/fields/pallas_call | solution.py:307
  43.0 9.9 %all_to_all.22 = bf16[32,16,128]{2,1,0:T(8,128)(2,1)S(1)} all-to-all(bf16[32,16,128]{2,1,0:T(8,128)(2,1)S(1)} %get-tuple-element.4), channel_id=1, replica_groups=mesh['groups'=2,'tile'=16] {'groups','tile'}, dimensions={0} | all-to-all | bytes 262144 | tf_op jit(solution)/shard_map/all_to_all | solution.py:318
  52.9 7.8 %potential.1 = bf16[512,256]{1,0:T(8,128)(2,1)S(1)} custom-call(bf16[512,128]{1,0:T(8,128)(2,1)S(1)} %bitcast.15, bf16[31,2048,256]{2,1,0:T(8,128)(2,1)} %chol_ref.3), custom_call_target="tpu_custom_call" | custom-call | flops 536870912 | bytes 16777216 | tf_op jit(solution)/shard_map/potential/pallas_call | solution.py:319
  60.7 12.0 %all_to_all.23 = bf16[32,16,256]{2,1,0:T(8,128)(2,1)S(1)} all-to-all(bf16[32,16,256]{2,1,0:T(8,128)(2,1)S(1)} %bitcast.12), channel_id=1, replica_groups=mesh['groups'=2,'tile'=16] {'groups','tile'}, dimensions={0} | all-to-all | bytes 524288 | tf_op jit(solution)/shard_map/all_to_all | solution.py:337
  72.6 0.0 copy-done
  72.6 0.0 copy-done.3
  72.6 0.0 copy-done.4
  72.6 3.7 %advance.1 = bf16[512,256]{1,0:T(8,128)(2,1)} custom-call(s32[16]{0:T(128)S(1)} %copy-done.4, s32[1,256]{1,0:T(1,128)S(1)} %bitcast.19, bf16[512,256]{1,0:T(8,128)(2,1)S(1)} %bitcast.13, bf16[512,256]{1,0:T(8,128)(2,1)S(1)} %bitcast.16), custom_call_target="tpu_custom_call" | custom-call | tf_op jit(solution)/shard_map/advance/pallas_call | solution.py:340
Async XLA Ops:
  0.6 41.1 %copy-start.1 = (s32[16,2048]{1,0:T(8,128)S(1)}, s32[16,2048]{1,0:T(8,128)}, u32[]{:S(2)}) copy-start(s32[16,2048]{1,0:T(8,128)} %aux_ref.1) | copy-start | bytes 393220
  0.6 41.1 %copy-start.5 = (f32[4]{0:T(128)S(1)}, f32[4]{0:T(128)}, u32[]{:S(2)}) copy-start(f32[4]{0:T(128)} %weight_ref.1) | copy-start | bytes 52
  0.7 41.1 %copy-start.2 = (s32[2048]{0:T(1024)S(1)}, s32[2048]{0:T(1024)}, u32[]{:S(2)}) copy-start(s32[2048]{0:T(1024)} %param.15) | copy-start | bytes 24580
  21.8 50.8 %copy-start = (bf16[1,512,256]{2,1,0:T(8,128)(2,1)S(1)}, bf16[1,512,256]{2,1,0:T(8,128)(2,1)}, u32[]{:S(2)}) copy-start(bf16[1,512,256]{2,1,0:T(8,128)(2,1)} %param.9) | copy-start | bytes 786436
  21.8 50.8 %copy-start.3 = (s32[256]{0:T(256)S(1)}, s32[256]{0:T(256)}, u32[]{:S(2)}) copy-start(s32[256]{0:T(256)} %param.13) | copy-start | bytes 3076
  21.8 50.8 %copy-start.4 = (s32[16]{0:T(128)S(1)}, s32[16]{0:T(128)}, u32[]{:S(2)}) copy-start(s32[16]{0:T(128)} %counts_ref.3) | copy-start | bytes 196

commit v2 on v1

--- a/solution.py
+++ b/solution.py
@@ -54,12 +54,16 @@
     return slot
 
 
-def tile_columns(pattern_ref, tiles, nblk, side):
-    pat = jnp.broadcast_to(pattern_ref[...].astype(F32), (LANES, tiles)).T.astype(jnp.int32)
+def row_of(pat, nblk, side):
     row_block = pat >> log2(nblk)
     col_block = pat & (nblk - 1)
     per = LANES // side
     return ((col_block >> log2(per)) << log2(nblk)) + row_block, col_block & (per - 1)
+
+
+def tile_columns(pattern_ref, tiles, nblk, side):
+    pat = jnp.broadcast_to(pattern_ref[...].astype(F32), (LANES, tiles)).T.astype(jnp.int32)
+    return row_of(pat, nblk, side)
 
 
 def green_kernel(
@@ -108,50 +112,40 @@
     return jnp.minimum(lax.axis_index("groups") * half, cap - half)
 
 
-def block_sizes(vectors):
-    if vectors % 1024:
-        return [vectors]
-    return [512] * (vectors // 512 - 1) + [256, 256]
-
-
-def bias_kernel(green_ref, chol_ref, out_ref, tall, left, back, held, sems, *, walkers, half):
+def bias_kernel(green_ref, chol_ref, out_ref, tall, left, back, held, sems, *, walkers, half, block):
     entries = green_ref.shape[1]
     vectors = held.shape[1]
     lanes = vectors // LANES
     narrow = entries // LANES
+    steps = vectors // block
     first = first_slot(half, chol_ref.shape[0])
-    blocks = block_sizes(vectors)
-    starts = [sum(blocks[:s]) for s in range(len(blocks))]
-    part = half // 4 if half % 4 == 0 else 1
-    copies = [
-        [
-            pltpu.make_async_copy(
-                chol_ref.at[pl.ds(first + j, part), pl.ds(at, size), :],
-                held.at[pl.ds(j, part), pl.ds(at, size), :],
-                sems.at[s, j // part],
-            )
-            for j in range(0, half, part)
-        ]
-        for s, (at, size) in enumerate(zip(starts, blocks))
-    ]
-    for group in copies:
-        for copy in group:
-            copy.start()
+
+    def fetch(s):
+        rows = pl.ds(s * block if isinstance(s, int) else pl.multiple_of(s * block, block), block)
+        return pltpu.make_async_copy(
+            chol_ref.at[pl.ds(first, half), rows, :], held.at[:, rows, :], sems.at[s]
+        )
+
+    for s in range(steps):
+        fetch(s).start()
     for k in range(narrow):
         tall[k] = green_ref[:, k * LANES : (k + 1) * LANES].astype(F32)
     for j in range(half):
         for k in range(narrow):
             at = j * entries + k * LANES
             left[:, at : at + LANES] = tall[k, pl.ds(j, walkers, stride=half), :].astype(BF)
-    for at, size, group in zip(starts, blocks, copies):
-        for copy in group:
-            copy.wait()
-        right = jnp.concatenate([held[j, at : at + size, :] for j in range(half)], axis=1)
+
+    def step(s, carry):
+        fetch(s).wait()
+        rows = pl.ds(pl.multiple_of(s * block, block), block)
+        right = jnp.concatenate([held[j, rows, :] for j in range(half)], axis=1)
         total = nt(left[...], right)
-        for i in range(size // LANES):
-            back[pl.ds(at // LANES + i, walkers, stride=lanes), :] = total[
-                :, i * LANES : (i + 1) * LANES
-            ]
+        for i in range(block // LANES):
+            place = s * (block // LANES) + i
+            back[pl.ds(place, walkers, stride=lanes), :] = total[:, i * LANES : (i + 1) * LANES]
+        return carry
+
+    lax.fori_loop(0, steps, step, 0)
     out_ref[...] = back[...].astype(BF)
 
 
@@ -181,55 +175,64 @@
     lanes = left.shape[1] // LANES
     narrow = entries // LANES
     first = first_slot(half, chol_ref.shape[0])
-    copies = [
-        pltpu.make_async_copy(chol_ref.at[first + j], held.at[j], sems.at[j]) for j in range(half)
-    ]
-    for copy in copies:
-        copy.start()
+
+    def fetch(j):
+        return pltpu.make_async_copy(chol_ref.at[first + j], held.at[j], sems.at[j])
+
+    def begin(j, carry):
+        fetch(j).start()
+        return carry
+
+    lax.fori_loop(0, half, begin, 0)
     tall[...] = fields_ref[...].astype(F32)
     for i in range(lanes):
         left[:, i * LANES : (i + 1) * LANES] = tall[pl.ds(i, walkers, stride=lanes), :].astype(BF)
-    for j in range(half):
-        copies[j].wait()
+
+    def step(j, carry):
+        fetch(j).wait()
         tile = mm(left[...], held[j])
         for k in range(narrow):
             back[k, pl.ds(j, walkers, stride=half), :] = tile[:, k * LANES : (k + 1) * LANES]
+        return carry
+
+    lax.fori_loop(0, half, step, 0)
     for k in range(narrow):
         out_ref[:, k * LANES : (k + 1) * LANES] = back[k].astype(BF)
 
 
+def prepare_kernel(
+    counts_ref, pattern_ref, after_ref, place_ref, spread_ref, pick_ref, inside_ref, *, owners, groups, half, cap, side, nblk
+):
+    del after_ref
+    tiles, slots = place_ref.shape
+    slot = slot_of_tile(counts_ref, tiles, owners, groups, half, cap)
+    slot = jnp.broadcast_to(slot.astype(F32), (LANES, tiles)).T.astype(jnp.int32)
+    lane = iota((tiles, LANES), 1)
+    for k in range(slots // LANES):
+        place_ref[:, k * LANES : (k + 1) * LANES] = one_hot(slot == lane + k * LANES)
+    src = iota(spread_ref.shape, 0)
+    dst = iota(spread_ref.shape, 1)
+    spread_ref[...] = one_hot(((dst >> log2(LANES)) << log2(side)) + (dst & (side - 1)) == src)
+    where_row, _ = row_of(pattern_ref[...], nblk, side)
+    pick_ref[...] = one_hot(iota((LANES, tiles), 0) == where_row)
+    _, place = tile_columns(pattern_ref, tiles, nblk, side)
+    inside_ref[...] = jnp.where(place == (lane >> log2(side)), 1.0, 0.0)
+
+
 def advance_kernel(
-    counts_ref, pattern_ref, tiles_ref, walker_ref, out_ref, wide_ref, *, owners, groups, half, cap, side
+    tiles_ref, place_ref, spread_ref, pick_ref, inside_ref, walker_ref, out_ref, wide_ref, *, side
 ):
     orbitals = walker_ref.shape[0]
     nblk = orbitals // side
-    tiles = pattern_ref.shape[1]
     wide = orbitals // LANES
-    entries = side * side
-    slots = tiles_ref.shape[0]
-    slot = slot_of_tile(counts_ref, tiles, owners, groups, half, cap)
-    place_in = one_hot(iota((slots, tiles), 0) == slot)
-    values = lax.dot_general(
-        place_in, tiles_ref[...], (((0,), (0,)), ((), ())), preferred_element_type=F32
-    ).astype(BF)
-    src = iota((entries, side * LANES), 0)
-    dst = iota((entries, side * LANES), 1)
-    spread = one_hot(((dst >> log2(LANES)) << log2(side)) + (dst & (side - 1)) == src)
-    where_row, place = tile_columns(pattern_ref, tiles, nblk, side)
-    lane = iota((tiles, LANES), 1)
-    inside = place == (lane >> log2(side))
-    repeated = mm(values, spread)
+    values = mm(place_ref[...], tiles_ref[...]).astype(BF)
+    repeated = mm(values, spread_ref[...])
+    inside = inside_ref[...]
     kept = jnp.concatenate(
-        [
-            jnp.where(inside, repeated[:, p * LANES : (p + 1) * LANES], 0.0).astype(BF)
-            for p in range(side)
-        ],
+        [(repeated[:, p * LANES : (p + 1) * LANES] * inside).astype(BF) for p in range(side)],
         axis=1,
     )
-    pick = one_hot(where_row == lane)
-    cut = lax.dot_general(
-        pick, kept, (((0,), (0,)), ((), ())), preferred_element_type=F32
-    )
+    cut = mm(pick_ref[...], kept)
     for k in range(wide):
         for p in range(side):
             wide_ref[k, pl.ds(p, nblk, stride=side), :] = cut[
@@ -267,6 +270,7 @@
     )
     large = pltpu.CompilerParams(vmem_limit_bytes=60 * 1024 * 1024)
     sizes = dict(owners=owners, groups=groups, half=half, cap=cap, side=side)
+    block = min(256, vectors)
     tile_bytes = half * vectors * entries * 2
     flops = 2 * devices * half * vectors * entries
     wide_scratch = pltpu.VMEM((orbitals // LANES, orbitals, LANES), F32)
@@ -284,7 +288,7 @@
         outgoing.reshape(devices, half, entries), both, split_axis=0, concat_axis=0
     )
     partial_bias = pl.pallas_call(
-        functools.partial(bias_kernel, walkers=devices, half=half),
+        functools.partial(bias_kernel, walkers=devices, half=half, block=block),
         out_shape=jax.ShapeDtypeStruct((devices * lanes, LANES), BF),
         in_specs=[vmem, hbm],
         out_specs=vmem,
@@ -293,7 +297,7 @@
             pltpu.VMEM((devices, half * entries), BF),
             pltpu.VMEM((devices * lanes, LANES), F32),
             pltpu.VMEM((half, vectors, entries), BF),
-            pltpu.SemaphoreType.DMA((len(block_sizes(vectors)), half)),
+            pltpu.SemaphoreType.DMA((vectors // block,)),
         ],
         compiler_params=streaming,
         cost_estimate=pl.CostEstimate(
@@ -337,15 +341,32 @@
     returned = lax.all_to_all(
         potential.reshape(devices, half, entries), both, split_axis=0, concat_axis=0
     )
+    spread_width = side * LANES
+    prepared = pl.pallas_call(
+        functools.partial(prepare_kernel, nblk=orbitals // side, **sizes),
+        out_shape=(
+            jax.ShapeDtypeStruct((tiles, devices * half), BF),
+            jax.ShapeDtypeStruct((entries, spread_width), BF),
+            jax.ShapeDtypeStruct((LANES, tiles), BF),
+            jax.ShapeDtypeStruct((tiles, LANES), F32),
+        ),
+        in_specs=[smem, vmem, hbm],
+        out_specs=(vmem, vmem, vmem, vmem),
+        compiler_params=params,
+        cost_estimate=pl.CostEstimate(
+            flops=10 * entries * spread_width, transcendentals=0, bytes_accessed=1 << 22
+        ),
+        name="prepare",
+    )(owner_counts, pattern_row, potential)
     advanced = pl.pallas_call(
-        functools.partial(advance_kernel, **sizes),
+        functools.partial(advance_kernel, side=side),
         out_shape=jax.ShapeDtypeStruct((orbitals, electrons), BF),
-        in_specs=[smem, vmem, vmem, vmem],
+        in_specs=[vmem] * 6,
         out_specs=vmem,
         scratch_shapes=[wide_scratch],
         compiler_params=params,
         name="advance",
-    )(owner_counts, pattern_row, returned.reshape(devices * half, entries), walkers[0])
+    )(returned.reshape(devices * half, entries), *prepared, walkers[0])
     return advanced[None], log_weight
 
 

time: 76.6 us -> 74.3 us (0.970)
  blocking collectives: 50 us -> 38 us
  waiting for transfers between devices: 0 us -> 9.04 us
  starting transfers between devices: 0 us -> 2.6 us
  Pallas kernels: 25.6 us -> 23.5 us
    all_to_all x1 -> x0, blocking collectives: 12 us -> none  [per_device(): lax.all_to_all(potential.reshape(devices, half, entries), both, split_axi...]
    all_to_all x0 -> x1, waiting for transfers between devices: none -> 9.04 us  [per_device(): lax.all_to_all(potential.reshape(devices, half, entries), both, split_axi...]
    all_to_all x0 -> x1, starting transfers between devices: none -> 2.6 us  [per_device(): lax.all_to_all(potential.reshape(devices, half, entries), both, split_axi...]
    pallas_call x2 -> x3, Pallas kernels: 13.1 us -> 11.8 us  [the longest x1 7.54 us: per_device(): pl.pallas_call(functools.partial(bias_kernel, walkers=devices, half=half,...]
    pallas_call x1, Pallas kernels: 7.78 us -> 6.99 us  [per_device(): pl.pallas_call(functools.partial(potential_kernel, walkers=devices, half=...]
  transfers between devices with their start and end apart: 0 -> 1, of which waited for: 0 -> 1; matrix products, arithmetic and copies ran while one was open for 0% -> 0% of each run, Pallas kernels for 0% -> 2%
where the time goes in v2:
time: 74.3 us; the launch traced here: 73.9 us
  blocking collectives  38 us (51%)
  Pallas kernels  23.5 us (32%)
  waiting for transfers between devices  9.04 us (12%)
  starting transfers between devices  2.6 us (3%)
    all_to_all x1, blocking collectives, per_device(): lax.all_to_all(outgoing.reshape(devices, half, entries), both, split_axis...  17.6 us
    all_to_all x1, blocking collectives, per_device(): lax.all_to_all(partial_bias.reshape(devices, lanes, LANES), both, split_a...  10.5 us
    all_to_all x1, blocking collectives, per_device(): fields = lax.all_to_all(fields, both, split_axis=0, concat_axis=0)  9.91 us
    all_to_all x1, waiting for transfers between devices, per_device(): lax.all_to_all(potential.reshape(devices, half, entries), both, split_axi...  9.04 us
    pallas_call x1, Pallas kernels, per_device(): pl.pallas_call(functools.partial(bias_kernel, walkers=devices, half=half,...  7.54 us
    pallas_call x1, Pallas kernels, per_device(): pl.pallas_call(functools.partial(potential_kernel, walkers=devices, half=...  6.99 us
    pallas_call x1, Pallas kernels, per_device(): pl.pallas_call(functools.partial(green_kernel, **sizes), out_shape=jax.Sh...  3.55 us
    pallas_call x1, Pallas kernels, per_device(): pl.pallas_call(functools.partial(advance_kernel, side=side), out_shape=ja...  3.04 us
  transfers between devices with their start and end apart: 1, of which 1 were waited for; matrix products, arithmetic and copies ran while one was open for 0% of the time, Pallas kernels for 2%

profile of v2, /device:TPU:0, one launch (start us, length us, event | category | flops | bytes accessed | tf_op | source)
XLA Modules:
  0.0 73.9 jit_solution(6899577509580315902)
XLA Ops:
  0.6 0.0 copy-start.1
  0.6 0.0 copy-start.5
  0.7 0.0 copy-start.2
  0.7 3.6 %green.1 = bf16[512,256]{1,0:T(8,128)(2,1)} custom-call(s32[16]{0:T(128)} %counts_ref.3, s32[1,256]{1,0:T(1,128)} %bitcast.17, bf16[512,256]{1,0:T(8,128)(2,1)} %bitcast.21, bf16[512,256]{1,0:T(8,128)(2,1)} %trial_ref.1), custom_call_target="tpu_custom_call" | custom-call | tf_op jit(solution)/shard_map/green/pallas_call | solution.py:278
  4.2 17.6 %all_to_all.20 = bf16[32,16,256]{2,1,0:T(8,128)(2,1)S(1)} all-to-all(bf16[32,16,256]{2,1,0:T(8,128)(2,1)} %bitcast.19), channel_id=1, replica_groups=mesh['groups'=2,'tile'=16] {'groups','tile'}, dimensions={0} | all-to-all | bytes 524288 | tf_op jit(solution)/shard_map/all_to_all | solution.py:287
  21.8 0.0 copy-start.3
  21.8 0.0 copy-start.4
  21.8 0.0 copy-start
  21.8 7.5 %bias.1 = bf16[512,128]{1,0:T(8,128)(2,1)S(1)} custom-call(bf16[512,256]{1,0:T(8,128)(2,1)S(1)} %bitcast.11, bf16[31,2048,256]{2,1,0:T(8,128)(2,1)} %chol_ref.3), custom_call_target="tpu_custom_call" | custom-call | flops 536870912 | bytes 16777216 | tf_op jit(solution)/shard_map/bias/pallas_call | solution.py:290
  29.4 10.5 %all_to_all.21.partial_ref = bf16[32,16,128]{2,1,0:T(8,128)(2,1)S(1)} all-to-all(bf16[32,16,128]{2,1,0:T(8,128)(2,1)S(1)} %bitcast.13), channel_id=1, replica_groups=mesh['groups'=2,'tile'=16] {'groups','tile'}, dimensions={0} | all-to-all | bytes 262144 | tf_op jit(solution)/shard_map/all_to_all | solution.py:308
  39.9 0.0 copy-done.1
  39.9 0.0 copy-done.5
  39.9 0.0 copy-done.2
  39.9 1.2 %fields.1 = (bf16[32,16,128]{2,1,0:T(8,128)(2,1)S(1)}, f32[1]{0:T(128)}) custom-call(f32[4]{0:T(128)S(1)} %copy-done.5, bf16[32,16,128]{2,1,0:T(8,128)(2,1)S(1)} %all_to_all.21.partial_ref, s32[16,2048]{1,0:T(8,128)S(1)} %copy-done.1, s32[16,128]{1,0:T(8,128)S(1)} %bitcast.16), custom_call_target="tpu_custom_call" | custom-call | tf_op jit(solution)/shard_map/fields/pallas_call | solution.py:311
  41.1 9.9 %all_to_all.22 = bf16[32,16,128]{2,1,0:T(8,128)(2,1)S(1)} all-to-all(bf16[32,16,128]{2,1,0:T(8,128)(2,1)S(1)} %get-tuple-element.8), channel_id=1, replica_groups=mesh['groups'=2,'tile'=16] {'groups','tile'}, dimensions={0} | all-to-all | bytes 262144 | tf_op jit(solution)/shard_map/all_to_all | solution.py:322
  51.0 7.0 %potential.1.after_ref = bf16[512,256]{1,0:T(8,128)(2,1)} custom-call(bf16[512,128]{1,0:T(8,128)(2,1)S(1)} %bitcast.14, bf16[31,2048,256]{2,1,0:T(8,128)(2,1)} %chol_ref.3), custom_call_target="tpu_custom_call" | custom-call | flops 536870912 | bytes 16777216 | tf_op jit(solution)/shard_map/potential/pallas_call | solution.py:323
  58.0 2.6 %all-to-all-start.3 = ((bf16[32,16,256]{2,1,0:T(8,128)(2,1)}), bf16[32,16,256]{2,1,0:T(8,128)(2,1)S(1)}, u32[]{:S(2)}, u32[]{:S(2)}) async-start(bf16[32,16,256]{2,1,0:T(8,128)(2,1)} %bitcast.7), calls=%async_computation.3 | async-start | bytes 524288 | tf_op jit(solution)/shard_map/all_to_all | solution.py:341
  60.6 0.0 copy-done.3
  60.7 0.0 copy-done.4
  60.7 1.2 %prepare.1 = (bf16[256,512]{1,0:T(8,128)(2,1)S(1)}, bf16[256,2048]{1,0:T(8,128)(2,1)S(1)}, bf16[128,256]{1,0:T(8,128)(2,1)S(1)}, f32[256,128]{1,0:T(8,128)S(1)}) custom-call(s32[16]{0:T(128)S(1)} %copy-done.4, s32[1,256]{1,0:T(1,128)S(1)} %bitcast.18, bf16[512,256]{1,0:T(8,128)(2,1)} %potential.1.after_ref), custom_call_target="tpu_custom_call" | custom-call | flops 5242880 | bytes 4194304 | tf_op jit(solution)/shard_map/prepare/pallas_call | solution.py:345
  61.9 9.0 %all-to-all-done.3 = bf16[32,16,256]{2,1,0:T(8,128)(2,1)S(1)} async-done(((bf16[32,16,256]{2,1,0:T(8,128)(2,1)}), bf16[32,16,256]{2,1,0:T(8,128)(2,1)S(1)}, u32[]{:S(2)}, u32[]{:S(2)}) %all-to-all-start.3) | async-done | bytes 262176 | tf_op jit(solution)/shard_map/all_to_all | solution.py:341
  70.9 0.0 copy-done
  70.9 3.0 %advance.1 = bf16[512,256]{1,0:T(8,128)(2,1)} custom-call(bf16[512,256]{1,0:T(8,128)(2,1)S(1)} %bitcast.12, bf16[256,512]{1,0:T(8,128)(2,1)S(1)} %get-tuple-element.9.place_ref, bf16[256,2048]{1,0:T(8,128)(2,1)S(1)} %get-tuple-element.10.spread_ref, bf16[128,256]{1,0:T(8,128)(2,1)S(1)} %get-tuple-element.11.pick_ref, ...), custom_call_target="tpu_custom_call" | custom-call | tf_op jit(solution)/shard_map/advance/pallas_call | solution.py:361
Async XLA Ops:
  0.6 39.3 %copy-start.1 = (s32[16,2048]{1,0:T(8,128)S(1)}, s32[16,2048]{1,0:T(8,128)}, u32[]{:S(2)}) copy-start(s32[16,2048]{1,0:T(8,128)} %aux_ref.1) | copy-start | bytes 393220
  0.6 39.3 %copy-start.5 = (f32[4]{0:T(128)S(1)}, f32[4]{0:T(128)}, u32[]{:S(2)}) copy-start(f32[4]{0:T(128)} %weight_ref.1) | copy-start | bytes 52
  0.7 39.3 %copy-start.2 = (s32[2048]{0:T(1024)S(1)}, s32[2048]{0:T(1024)}, u32[]{:S(2)}) copy-start(s32[2048]{0:T(1024)} %param.15) | copy-start | bytes 24580
  21.8 38.8 %copy-start.3 = (s32[256]{0:T(256)S(1)}, s32[256]{0:T(256)}, u32[]{:S(2)}) copy-start(s32[256]{0:T(256)} %param.13) | copy-start | bytes 3076
  21.8 38.9 %copy-start.4 = (s32[16]{0:T(128)S(1)}, s32[16]{0:T(128)}, u32[]{:S(2)}) copy-start(s32[16]{0:T(128)} %counts_ref.3) | copy-start | bytes 196
  21.8 49.1 %copy-start = (bf16[1,512,256]{2,1,0:T(8,128)(2,1)S(1)}, bf16[1,512,256]{2,1,0:T(8,128)(2,1)}, u32[]{:S(2)}) copy-start(bf16[1,512,256]{2,1,0:T(8,128)(2,1)} %param.9) | copy-start | bytes 786436
  58.0 12.9 %all-to-all-start.3 = ((bf16[32,16,256]{2,1,0:T(8,128)(2,1)}), bf16[32,16,256]{2,1,0:T(8,128)(2,1)S(1)}, u32[]{:S(2)}, u32[]{:S(2)}) async-start(bf16[32,16,256]{2,1,0:T(8,128)(2,1)} %bitcast.7), calls=%async_computation.3 | async-start | bytes 524288 | tf_op jit(solution)/shard_map/all_to_all | solution.py:341

commit v3 on v2

--- a/solution.py
+++ b/solution.py
@@ -67,13 +67,42 @@
 
 
 def green_kernel(
-    counts_ref, pattern_ref, factor_ref, trial_ref, out_ref, wide_ref, *, owners, groups, half, cap, side
-):
+    counts_hbm, pattern_hbm, factor_hbm, trial_hbm, out_ref,
+    counts_ref, pattern_ref, factor_ref, trial_ref, wide_ref, fold_ref, slot_ref, sems,
+    *, owners, groups, half, cap, side,
+):
+    copies = [
+        pltpu.make_async_copy(source, held, sems.at[i])
+        for i, (source, held) in enumerate(
+            [
+                (counts_hbm, counts_ref),
+                (pattern_hbm, pattern_ref),
+                (factor_hbm, factor_ref),
+                (trial_hbm, trial_ref),
+            ]
+        )
+    ]
+    for copy in copies:
+        copy.start()
     orbitals = factor_ref.shape[0]
     nblk = orbitals // side
     tiles = pattern_ref.shape[1]
+    slots = out_ref.shape[0]
     wide = orbitals // LANES
     assert wide * nblk == LANES
+    src = iota(fold_ref.shape, 0)
+    dst = iota(fold_ref.shape, 1)
+    fold_ref[...] = one_hot(((src >> log2(LANES)) << log2(side)) + (src & (side - 1)) == dst)
+    copies[0].wait()
+    copies[1].wait()
+    where_row, place = tile_columns(pattern_ref, tiles, nblk, side)
+    lane = iota((tiles, LANES), 1)
+    pick = one_hot(where_row == lane)
+    inside = place == (lane >> log2(side))
+    slot = slot_of_tile(counts_ref, tiles, owners, groups, half, cap)
+    slot_ref[...] = one_hot(iota((slots, tiles), 0) == slot)
+    copies[2].wait()
+    copies[3].wait()
     green = nt(factor_ref[...], trial_ref[...])
     for k in range(wide):
         wide_ref[k] = green[:, k * LANES : (k + 1) * LANES]
@@ -86,10 +115,6 @@
         ],
         axis=0,
     )
-    where_row, place = tile_columns(pattern_ref, tiles, nblk, side)
-    lane = iota((tiles, LANES), 1)
-    pick = one_hot(where_row == lane)
-    inside = place == (lane >> log2(side))
     found = mm(pick, cut)
     kept = jnp.concatenate(
         [
@@ -98,14 +123,12 @@
         ],
         axis=1,
     )
-    entries = side * side
-    src = iota((side * LANES, entries), 0)
-    dst = iota((side * LANES, entries), 1)
-    fold = one_hot(((src >> log2(LANES)) << log2(side)) + (src & (side - 1)) == dst)
-    values = mm(kept, fold).astype(BF)
-    slot = slot_of_tile(counts_ref, tiles, owners, groups, half, cap)
-    slots = out_ref.shape[0]
-    out_ref[...] = mm(one_hot(iota((slots, tiles), 0) == slot), values).astype(BF)
+    values = mm(kept, fold_ref[...]).astype(BF)
+    out_ref[...] = mm(slot_ref[...], values).astype(BF)
+
+
+def in_place(x):
+    return pltpu.with_memory_space_constraint(x, pltpu.HBM)
 
 
 def first_slot(half, cap):
@@ -170,44 +193,13 @@
     logw_ref[0] = jnp.sum(sampled * bias - 0.5 * bias * bias)
 
 
-def potential_kernel(fields_ref, chol_ref, out_ref, tall, left, back, held, sems, *, walkers, half):
-    entries = held.shape[2]
-    lanes = left.shape[1] // LANES
-    narrow = entries // LANES
-    first = first_slot(half, chol_ref.shape[0])
-
-    def fetch(j):
-        return pltpu.make_async_copy(chol_ref.at[first + j], held.at[j], sems.at[j])
-
-    def begin(j, carry):
-        fetch(j).start()
-        return carry
-
-    lax.fori_loop(0, half, begin, 0)
-    tall[...] = fields_ref[...].astype(F32)
-    for i in range(lanes):
-        left[:, i * LANES : (i + 1) * LANES] = tall[pl.ds(i, walkers, stride=lanes), :].astype(BF)
-
-    def step(j, carry):
-        fetch(j).wait()
-        tile = mm(left[...], held[j])
-        for k in range(narrow):
-            back[k, pl.ds(j, walkers, stride=half), :] = tile[:, k * LANES : (k + 1) * LANES]
-        return carry
-
-    lax.fori_loop(0, half, step, 0)
-    for k in range(narrow):
-        out_ref[:, k * LANES : (k + 1) * LANES] = back[k].astype(BF)
-
-
-def prepare_kernel(
-    counts_ref, pattern_ref, after_ref, place_ref, spread_ref, pick_ref, inside_ref, *, owners, groups, half, cap, side, nblk
-):
-    del after_ref
+def prepare(
+    counts_ref, pattern_ref, place_ref, spread_ref, pick_ref, inside_ref, *, owners, groups, half, cap, side, nblk
+):
     tiles, slots = place_ref.shape
+    lane = iota((tiles, LANES), 1)
     slot = slot_of_tile(counts_ref, tiles, owners, groups, half, cap)
     slot = jnp.broadcast_to(slot.astype(F32), (LANES, tiles)).T.astype(jnp.int32)
-    lane = iota((tiles, LANES), 1)
     for k in range(slots // LANES):
         place_ref[:, k * LANES : (k + 1) * LANES] = one_hot(slot == lane + k * LANES)
     src = iota(spread_ref.shape, 0)
@@ -217,6 +209,43 @@
     pick_ref[...] = one_hot(iota((LANES, tiles), 0) == where_row)
     _, place = tile_columns(pattern_ref, tiles, nblk, side)
     inside_ref[...] = jnp.where(place == (lane >> log2(side)), 1.0, 0.0)
+
+
+def potential_kernel(
+    counts_ref, pattern_ref, fields_ref, chol_ref,
+    out_ref, place_ref, spread_ref, pick_ref, inside_ref,
+    tall, left, back, held, sems, *, walkers, half, **sizes,
+):
+    entries = held.shape[2]
+    lanes = left.shape[1] // LANES
+    narrow = entries // LANES
+    first = first_slot(half, chol_ref.shape[0])
+
+    def fetch(j):
+        return pltpu.make_async_copy(chol_ref.at[first + j], held.at[j], sems.at[j])
+
+    def begin(j, carry):
+        fetch(j).start()
+        return carry
+
+    lax.fori_loop(0, half, begin, 0)
+    prepare(
+        counts_ref, pattern_ref, place_ref, spread_ref, pick_ref, inside_ref, half=half, **sizes
+    )
+    tall[...] = fields_ref[...].astype(F32)
+    for i in range(lanes):
+        left[:, i * LANES : (i + 1) * LANES] = tall[pl.ds(i, walkers, stride=lanes), :].astype(BF)
+
+    def step(j, carry):
+        fetch(j).wait()
+        tile = mm(left[...], held[j])
+        for k in range(narrow):
+            back[k, pl.ds(j, walkers, stride=half), :] = tile[:, k * LANES : (k + 1) * LANES]
+        return carry
+
+    lax.fori_loop(0, half, step, 0)
+    for k in range(narrow):
+        out_ref[:, k * LANES : (k + 1) * LANES] = back[k].astype(BF)
 
 
 def advance_kernel(
@@ -265,10 +294,10 @@
     vmem = pl.BlockSpec(memory_space=pltpu.VMEM)
     params = pltpu.CompilerParams(vmem_limit_bytes=VMEM_LIMIT)
     hbm = pl.BlockSpec(memory_space=pl.ANY)
+    in_hbm = pl.BlockSpec(memory_space=pltpu.HBM)
     streaming = pltpu.CompilerParams(
         vmem_limit_bytes=VMEM_LIMIT + 2 * half * vectors * entries
     )
-    large = pltpu.CompilerParams(vmem_limit_bytes=60 * 1024 * 1024)
     sizes = dict(owners=owners, groups=groups, half=half, cap=cap, side=side)
     block = min(256, vectors)
     tile_bytes = half * vectors * entries * 2
@@ -278,12 +307,21 @@
     outgoing = pl.pallas_call(
         functools.partial(green_kernel, **sizes),
         out_shape=jax.ShapeDtypeStruct((devices * half, entries), BF),
-        in_specs=[smem, vmem, vmem, vmem],
+        in_specs=[in_hbm] * 4,
         out_specs=vmem,
-        scratch_shapes=[wide_scratch],
-        compiler_params=large,
+        scratch_shapes=[
+            pltpu.SMEM(owner_counts.shape, jnp.int32),
+            pltpu.VMEM((1, tiles), jnp.int32),
+            pltpu.VMEM((orbitals, electrons), BF),
+            pltpu.VMEM((orbitals, electrons), BF),
+            wide_scratch,
+            pltpu.VMEM((side * LANES, entries), BF),
+            pltpu.VMEM((devices * half, tiles), BF),
+            pltpu.SemaphoreType.DMA((4,)),
+        ],
+        compiler_params=params,
         name="green",
-    )(owner_counts, pattern_row, green_factor[0], trial)
+    )(*(in_place(x) for x in (owner_counts, pattern_row, green_factor[0], trial)))
     arrived = lax.all_to_all(
         outgoing.reshape(devices, half, entries), both, split_axis=0, concat_axis=0
     )
@@ -320,11 +358,20 @@
         name="fields",
     )(group_weight, partial_bias, aux, chol_group.reshape(lanes, LANES))
     fields = lax.all_to_all(fields, both, split_axis=0, concat_axis=0)
-    potential = pl.pallas_call(
-        functools.partial(potential_kernel, walkers=devices, half=half),
-        out_shape=jax.ShapeDtypeStruct((devices * half, entries), BF),
-        in_specs=[vmem, hbm],
-        out_specs=vmem,
+    spread_width = side * LANES
+    potential, *prepared = pl.pallas_call(
+        functools.partial(
+            potential_kernel, walkers=devices, nblk=orbitals // side, **sizes
+        ),
+        out_shape=(
+            jax.ShapeDtypeStruct((devices * half, entries), BF),
+            jax.ShapeDtypeStruct((tiles, devices * half), BF),
+            jax.ShapeDtypeStruct((entries, spread_width), BF),
+            jax.ShapeDtypeStruct((LANES, tiles), BF),
+            jax.ShapeDtypeStruct((tiles, LANES), F32),
+        ),
+        in_specs=[smem, vmem, vmem, hbm],
+        out_specs=(vmem,) * 5,
         scratch_shapes=[
             pltpu.VMEM((devices * lanes, LANES), F32),
             pltpu.VMEM((devices, vectors), BF),
@@ -337,27 +384,10 @@
             flops=flops, transcendentals=0, bytes_accessed=tile_bytes
         ),
         name="potential",
-    )(fields.reshape(devices * lanes, LANES), chol)
+    )(owner_counts, pattern_row, fields.reshape(devices * lanes, LANES), chol)
     returned = lax.all_to_all(
         potential.reshape(devices, half, entries), both, split_axis=0, concat_axis=0
     )
-    spread_width = side * LANES
-    prepared = pl.pallas_call(
-        functools.partial(prepare_kernel, nblk=orbitals // side, **sizes),
-        out_shape=(
-            jax.ShapeDtypeStruct((tiles, devices * half), BF),
-            jax.ShapeDtypeStruct((entries, spread_width), BF),
-            jax.ShapeDtypeStruct((LANES, tiles), BF),
-            jax.ShapeDtypeStruct((tiles, LANES), F32),
-        ),
-        in_specs=[smem, vmem, hbm],
-        out_specs=(vmem, vmem, vmem, vmem),
-        compiler_params=params,
-        cost_estimate=pl.CostEstimate(
-            flops=10 * entries * spread_width, transcendentals=0, bytes_accessed=1 << 22
-        ),
-        name="prepare",
-    )(owner_counts, pattern_row, potential)
     advanced = pl.pallas_call(
         functools.partial(advance_kernel, side=side),
         out_shape=jax.ShapeDtypeStruct((orbitals, electrons), BF),

time: 74.3 us -> 72.2 us (0.972)
  blocking collectives: 38 us -> 49.8 us
  waiting for transfers between devices: 9.04 us -> 0 us
  starting transfers between devices: 2.6 us -> 0 us
  Pallas kernels: 23.5 us -> 21.5 us
    all_to_all x0 -> x1, blocking collectives: none -> 12 us  [per_device(): lax.all_to_all(potential.reshape(devices, half, entries), both, split_axi...]
    all_to_all x1 -> x0, waiting for transfers between devices: 9.04 us -> none  [per_device(): lax.all_to_all(potential.reshape(devices, half, entries), both, split_axi...]
    all_to_all x1 -> x0, starting transfers between devices: 2.6 us -> none  [per_device(): lax.all_to_all(potential.reshape(devices, half, entries), both, split_axi...]
    pallas_call x2 -> x1, Pallas kernels: 8.18 us -> 6.85 us  [per_device(): pl.pallas_call(functools.partial(potential_kernel, walkers=devices, nblk=...]
  transfers between devices with their start and end apart: 1 -> 0, of which waited for: 1 -> 0; matrix products, arithmetic and copies ran while one was open for 0% -> 0% of each run, Pallas kernels for 2% -> 0%
where the time goes in v3:
time: 72.2 us; the launch traced here: 72 us
  blocking collectives  49.8 us (69%)
  Pallas kernels  21.5 us (30%)
    all_to_all x1, blocking collectives, per_device(): lax.all_to_all(outgoing.reshape(devices, half, entries), both, split_axis...  17.4 us
    all_to_all x1, blocking collectives, per_device(): lax.all_to_all(potential.reshape(devices, half, entries), both, split_axi...  12 us
    all_to_all x1, blocking collectives, per_device(): lax.all_to_all(partial_bias.reshape(devices, lanes, LANES), both, split_a...  10.5 us
    all_to_all x1, blocking collectives, per_device(): fields = lax.all_to_all(fields, both, split_axis=0, concat_axis=0)  9.91 us
    pallas_call x1, Pallas kernels, per_device(): pl.pallas_call(functools.partial(bias_kernel, walkers=devices, half=half,...  7.53 us
    pallas_call x1, Pallas kernels, per_device(): pl.pallas_call(functools.partial(potential_kernel, walkers=devices, nblk=...  6.85 us
    pallas_call x1, Pallas kernels, per_device(): pl.pallas_call(functools.partial(advance_kernel, side=side), out_shape=ja...  3.05 us
    pallas_call x1, Pallas kernels, per_device(): pl.pallas_call(functools.partial(green_kernel, **sizes), out_shape=jax.Sh...  2.86 us

profile of v3, /device:TPU:0, one launch (start us, length us, event | category | flops | bytes accessed | tf_op | source)
XLA Modules:
  0.0 72.0 jit_solution(10943967680839069881)
XLA Ops:
  0.6 0.0 copy-start.4
  0.6 0.0 copy-start.3
  0.7 0.0 copy-start.1
  0.7 0.0 copy-start.5
  0.7 0.0 copy-start.2
  0.7 2.9 %green.1 = bf16[512,256]{1,0:T(8,128)(2,1)S(1)} custom-call(s32[16]{0:T(128)} %counts_ref.1, s32[1,256]{1,0:T(1,128)} %bitcast.19, bf16[512,256]{1,0:T(8,128)(2,1)} %bitcast.22, bf16[512,256]{1,0:T(8,128)(2,1)} %trial_hbm.1), custom_call_target="tpu_custom_call" | custom-call | tf_op jit(solution)/shard_map/green/pallas_call | solution.py:307
  3.5 17.4 %all_to_all.20 = bf16[32,16,256]{2,1,0:T(8,128)(2,1)S(1)} all-to-all(bf16[32,16,256]{2,1,0:T(8,128)(2,1)S(1)} %bitcast.13), channel_id=1, replica_groups=mesh['groups'=2,'tile'=16] {'groups','tile'}, dimensions={0} | all-to-all | bytes 524288 | tf_op jit(solution)/shard_map/all_to_all | solution.py:325
  20.9 0.0 copy-start
  20.9 7.5 %bias.1 = bf16[512,128]{1,0:T(8,128)(2,1)S(1)} custom-call(bf16[512,256]{1,0:T(8,128)(2,1)S(1)} %bitcast.11, bf16[31,2048,256]{2,1,0:T(8,128)(2,1)} %chol_ref.3), custom_call_target="tpu_custom_call" | custom-call | flops 536870912 | bytes 16777216 | tf_op jit(solution)/shard_map/bias/pallas_call | solution.py:328
  28.5 10.5 %all_to_all.21.partial_ref = bf16[32,16,128]{2,1,0:T(8,128)(2,1)S(1)} all-to-all(bf16[32,16,128]{2,1,0:T(8,128)(2,1)S(1)} %bitcast.15), channel_id=1, replica_groups=mesh['groups'=2,'tile'=16] {'groups','tile'}, dimensions={0} | all-to-all | bytes 262144 | tf_op jit(solution)/shard_map/all_to_all | solution.py:346
  39.0 0.0 copy-done.1
  39.0 0.0 copy-done.5
  39.0 0.0 copy-done.2
  39.0 1.2 %fields.1 = (bf16[32,16,128]{2,1,0:T(8,128)(2,1)S(1)}, f32[1]{0:T(128)}) custom-call(f32[4]{0:T(128)S(1)} %copy-done.5, bf16[32,16,128]{2,1,0:T(8,128)(2,1)S(1)} %all_to_all.21.partial_ref, s32[16,2048]{1,0:T(8,128)S(1)} %copy-done.1, s32[16,128]{1,0:T(8,128)S(1)} %bitcast.18), custom_call_target="tpu_custom_call" | custom-call | tf_op jit(solution)/shard_map/fields/pallas_call | solution.py:349
  40.2 9.9 %all_to_all.22 = bf16[32,16,128]{2,1,0:T(8,128)(2,1)S(1)} all-to-all(bf16[32,16,128]{2,1,0:T(8,128)(2,1)S(1)} %get-tuple-element.9), channel_id=1, replica_groups=mesh['groups'=2,'tile'=16] {'groups','tile'}, dimensions={0} | all-to-all | bytes 262144 | tf_op jit(solution)/shard_map/all_to_all | solution.py:360
  50.2 0.0 copy-done.4
  50.2 0.0 copy-done.3
  50.2 6.9 %potential.1 = (bf16[512,256]{1,0:T(8,128)(2,1)S(1)}, bf16[256,512]{1,0:T(8,128)(2,1)S(1)}, bf16[256,2048]{1,0:T(8,128)(2,1)S(1)}, bf16[128,256]{1,0:T(8,128)(2,1)S(1)}, f32[256,128]{1,0:T(8,128)S(1)}) custom-call(s32[16]{0:T(128)S(1)} %copy-done.4, s32[1,256]{1,0:T(1,128)S(1)} %bitcast.20, bf16[512,128]{1,0:T(8,128)(2,1)S(1)} %bitcast.14, ...), custom_call_target="tpu_custom_call" | custom-call | flops 536870912 | bytes 16777216 | tf_op jit(solution)/shard_map/potential/pallas_call | solution.py:362
  57.0 12.0 %all_to_all.23 = bf16[32,16,256]{2,1,0:T(8,128)(2,1)S(1)} all-to-all(bf16[32,16,256]{2,1,0:T(8,128)(2,1)S(1)} %bitcast.17), channel_id=1, replica_groups=mesh['groups'=2,'tile'=16] {'groups','tile'}, dimensions={0} | all-to-all | bytes 524288 | tf_op jit(solution)/shard_map/all_to_all | solution.py:388
  69.0 0.0 copy-done
  69.0 3.0 %advance.1 = bf16[512,256]{1,0:T(8,128)(2,1)} custom-call(bf16[512,256]{1,0:T(8,128)(2,1)S(1)} %bitcast.12, bf16[256,512]{1,0:T(8,128)(2,1)S(1)} %get-tuple-element.11.place_ref, bf16[256,2048]{1,0:T(8,128)(2,1)S(1)} %get-tuple-element.12.spread_ref, bf16[128,256]{1,0:T(8,128)(2,1)S(1)} %get-tuple-element.13.pick_ref, ...), custom_call_target="tpu_custom_call" | custom-call | tf_op jit(solution)/shard_map/advance/pallas_call | solution.py:391
Async XLA Ops:
  0.6 49.5 %copy-start.4 = (s32[16]{0:T(128)S(1)}, s32[16]{0:T(128)}, u32[]{:S(2)}) copy-start(s32[16]{0:T(128)} %counts_ref.1) | copy-start | bytes 196
  0.6 49.5 %copy-start.3 = (s32[256]{0:T(256)S(1)}, s32[256]{0:T(256)}, u32[]{:S(2)}) copy-start(s32[256]{0:T(256)} %param.13) | copy-start | bytes 3076
  0.7 38.4 %copy-start.1 = (s32[16,2048]{1,0:T(8,128)S(1)}, s32[16,2048]{1,0:T(8,128)}, u32[]{:S(2)}) copy-start(s32[16,2048]{1,0:T(8,128)} %aux_ref.1) | copy-start | bytes 393220
  0.7 38.4 %copy-start.5 = (f32[4]{0:T(128)S(1)}, f32[4]{0:T(128)}, u32[]{:S(2)}) copy-start(f32[4]{0:T(128)} %weight_ref.1) | copy-start | bytes 52
  0.7 38.4 %copy-start.2 = (s32[2048]{0:T(1024)S(1)}, s32[2048]{0:T(1024)}, u32[]{:S(2)}) copy-start(s32[2048]{0:T(1024)} %param.15) | copy-start | bytes 24580
  20.9 48.1 %copy-start = (bf16[1,512,256]{2,1,0:T(8,128)(2,1)S(1)}, bf16[1,512,256]{2,1,0:T(8,128)(2,1)}, u32[]{:S(2)}) copy-start(bf16[1,512,256]{2,1,0:T(8,128)(2,1)} %param.9) | copy-start | bytes 786436

commit v4 on v3

--- a/solution.py
+++ b/solution.py
@@ -135,7 +135,25 @@
     return jnp.minimum(lax.axis_index("groups") * half, cap - half)
 
 
-def bias_kernel(green_ref, chol_ref, out_ref, tall, left, back, held, sems, *, walkers, half, block):
+def draw_row(aux_ref, group_ref, weight_ref, sampled_ref, scale_ref):
+    lanes = group_ref.shape[0]
+    draws = aux_ref[pl.ds(lax.axis_index("tile"), 1), :]
+    for i in range(lanes):
+        sampled_ref[i : i + 1, :] = draws[:, i * LANES : (i + 1) * LANES].astype(F32) * (
+            1.0 / 262144.0
+        )
+    scale = jnp.zeros(group_ref.shape, F32)
+    for k in range(weight_ref.shape[0]):
+        scale = jnp.where(group_ref[...] == k, weight_ref[k], scale)
+    scale_ref[...] = scale
+
+
+def bias_kernel(
+    green_ref, chol_ref, aux_hbm, group_hbm, weight_hbm,
+    out_ref, sampled_ref, scale_ref,
+    tall, left, back, held, aux_ref, group_ref, weight_ref, side_sems, sems,
+    *, walkers, half, block,
+):
     entries = green_ref.shape[1]
     vectors = held.shape[1]
     lanes = vectors // LANES
@@ -149,6 +167,14 @@
             chol_ref.at[pl.ds(first, half), rows, :], held.at[:, rows, :], sems.at[s]
         )
 
+    others = [
+        pltpu.make_async_copy(source, dest, side_sems.at[i])
+        for i, (source, dest) in enumerate(
+            [(aux_hbm, aux_ref), (group_hbm, group_ref), (weight_hbm, weight_ref)]
+        )
+    ]
+    for copy in others:
+        copy.start()
     for s in range(steps):
         fetch(s).start()
     for k in range(narrow):
@@ -157,6 +183,9 @@
         for k in range(narrow):
             at = j * entries + k * LANES
             left[:, at : at + LANES] = tall[k, pl.ds(j, walkers, stride=half), :].astype(BF)
+    for copy in others:
+        copy.wait()
+    draw_row(aux_ref, group_ref, weight_ref, sampled_ref, scale_ref)
 
     def step(s, carry):
         fetch(s).wait()
@@ -172,25 +201,15 @@
     out_ref[...] = back[...].astype(BF)
 
 
-def field_kernel(
-    weight_ref, partial_ref, aux_ref, group_ref, fields_ref, logw_ref, *, devices
-):
-    lanes = group_ref.shape[0]
-    bias = jnp.zeros((lanes, LANES), F32)
-    for i in range(devices):
+def field_kernel(partial_ref, sampled_ref, scale_ref, fields_ref, summand_ref, *, devices):
+    bias = partial_ref[0].astype(F32)
+    for i in range(1, devices):
         bias = bias + partial_ref[i].astype(F32)
-    draws = aux_ref[pl.ds(lax.axis_index("tile"), 1), :]
-    draws = jnp.concatenate(
-        [draws[:, i * LANES : (i + 1) * LANES] for i in range(lanes)], axis=0
-    )
-    sampled = draws.astype(F32) * (1.0 / 262144.0)
-    weight = jnp.zeros((lanes, LANES), F32)
-    for k in range(weight_ref.shape[0]):
-        weight = jnp.where(group_ref[...] == k, weight_ref[k], weight)
-    fields = (weight * (sampled - bias)).astype(BF)
+    sampled = sampled_ref[...]
+    fields = (scale_ref[...] * (sampled - bias)).astype(BF)
     for i in range(devices):
         fields_ref[i] = fields
-    logw_ref[0] = jnp.sum(sampled * bias - 0.5 * bias * bias)
+    summand_ref[...] = sampled * bias - 0.5 * bias * bias
 
 
 def prepare(
@@ -212,9 +231,9 @@
 
 
 def potential_kernel(
-    counts_ref, pattern_ref, fields_ref, chol_ref,
+    counts_hbm, pattern_ref, fields_ref, chol_ref,
     out_ref, place_ref, spread_ref, pick_ref, inside_ref,
-    tall, left, back, held, sems, *, walkers, half, **sizes,
+    tall, left, back, held, counts_ref, counts_sem, sems, *, walkers, half, **sizes,
 ):
     entries = held.shape[2]
     lanes = left.shape[1] // LANES
@@ -228,7 +247,10 @@
         fetch(j).start()
         return carry
 
+    counts = pltpu.make_async_copy(counts_hbm, counts_ref, counts_sem)
+    counts.start()
     lax.fori_loop(0, half, begin, 0)
+    counts.wait()
     prepare(
         counts_ref, pattern_ref, place_ref, spread_ref, pick_ref, inside_ref, half=half, **sizes
     )
@@ -249,8 +271,10 @@
 
 
 def advance_kernel(
-    tiles_ref, place_ref, spread_ref, pick_ref, inside_ref, walker_ref, out_ref, wide_ref, *, side
-):
+    tiles_ref, place_ref, spread_ref, pick_ref, inside_ref, walker_ref, summand_ref,
+    out_ref, logw_ref, wide_ref, *, side,
+):
+    logw_ref[0] = jnp.sum(summand_ref[...])
     orbitals = walker_ref.shape[0]
     nblk = orbitals // side
     wide = orbitals // LANES
@@ -325,16 +349,24 @@
     arrived = lax.all_to_all(
         outgoing.reshape(devices, half, entries), both, split_axis=0, concat_axis=0
     )
-    partial_bias = pl.pallas_call(
+    partial_bias, sampled, scale = pl.pallas_call(
         functools.partial(bias_kernel, walkers=devices, half=half, block=block),
-        out_shape=jax.ShapeDtypeStruct((devices * lanes, LANES), BF),
-        in_specs=[vmem, hbm],
-        out_specs=vmem,
+        out_shape=(
+            jax.ShapeDtypeStruct((devices * lanes, LANES), BF),
+            jax.ShapeDtypeStruct((lanes, LANES), F32),
+            jax.ShapeDtypeStruct((lanes, LANES), F32),
+        ),
+        in_specs=[vmem, hbm, in_hbm, in_hbm, in_hbm],
+        out_specs=(vmem,) * 3,
         scratch_shapes=[
             pltpu.VMEM((entries // LANES, half * devices, LANES), F32),
             pltpu.VMEM((devices, half * entries), BF),
             pltpu.VMEM((devices * lanes, LANES), F32),
             pltpu.VMEM((half, vectors, entries), BF),
+            pltpu.VMEM(aux.shape, jnp.int32),
+            pltpu.VMEM((lanes, LANES), jnp.int32),
+            pltpu.SMEM(group_weight.shape, F32),
+            pltpu.SemaphoreType.DMA((3,)),
             pltpu.SemaphoreType.DMA((vectors // block,)),
         ],
         compiler_params=streaming,
@@ -342,21 +374,27 @@
             flops=flops, transcendentals=0, bytes_accessed=tile_bytes
         ),
         name="bias",
-    )(arrived.reshape(devices * half, entries), chol)
+    )(
+        arrived.reshape(devices * half, entries),
+        chol,
+        in_place(aux),
+        in_place(chol_group.reshape(lanes, LANES)),
+        in_place(group_weight),
+    )
     partial_bias = lax.all_to_all(
         partial_bias.reshape(devices, lanes, LANES), both, split_axis=0, concat_axis=0
     )
-    fields, log_weight = pl.pallas_call(
+    fields, summand = pl.pallas_call(
         functools.partial(field_kernel, devices=devices),
         out_shape=(
             jax.ShapeDtypeStruct((devices, lanes, LANES), BF),
-            jax.ShapeDtypeStruct((1,), F32),
-        ),
-        in_specs=[smem, vmem, vmem, vmem],
-        out_specs=(vmem, smem),
+            jax.ShapeDtypeStruct((lanes, LANES), F32),
+        ),
+        in_specs=[vmem] * 3,
+        out_specs=(vmem,) * 2,
         compiler_params=params,
         name="fields",
-    )(group_weight, partial_bias, aux, chol_group.reshape(lanes, LANES))
+    )(partial_bias, sampled, scale)
     fields = lax.all_to_all(fields, both, split_axis=0, concat_axis=0)
     spread_width = side * LANES
     potential, *prepared = pl.pallas_call(
@@ -370,13 +408,15 @@
             jax.ShapeDtypeStruct((LANES, tiles), BF),
             jax.ShapeDtypeStruct((tiles, LANES), F32),
         ),
-        in_specs=[smem, vmem, vmem, hbm],
+        in_specs=[in_hbm, vmem, vmem, hbm],
         out_specs=(vmem,) * 5,
         scratch_shapes=[
             pltpu.VMEM((devices * lanes, LANES), F32),
             pltpu.VMEM((devices, vectors), BF),
             pltpu.VMEM((entries // LANES, half * devices, LANES), F32),
             pltpu.VMEM((half, vectors, entries), BF),
+            pltpu.SMEM(owner_counts.shape, jnp.int32),
+            pltpu.SemaphoreType.DMA,
             pltpu.SemaphoreType.DMA((half,)),
         ],
         compiler_params=streaming,
@@ -384,19 +424,22 @@
             flops=flops, transcendentals=0, bytes_accessed=tile_bytes
         ),
         name="potential",
-    )(owner_counts, pattern_row, fields.reshape(devices * lanes, LANES), chol)
+    )(in_place(owner_counts), pattern_row, fields.reshape(devices * lanes, LANES), chol)
     returned = lax.all_to_all(
         potential.reshape(devices, half, entries), both, split_axis=0, concat_axis=0
     )
-    advanced = pl.pallas_call(
+    advanced, log_weight = pl.pallas_call(
         functools.partial(advance_kernel, side=side),
-        out_shape=jax.ShapeDtypeStruct((orbitals, electrons), BF),
-        in_specs=[vmem] * 6,
-        out_specs=vmem,
+        out_shape=(
+            jax.ShapeDtypeStruct((orbitals, electrons), BF),
+            jax.ShapeDtypeStruct((1,), F32),
+        ),
+        in_specs=[vmem] * 7,
+        out_specs=(vmem, smem),
         scratch_shapes=[wide_scratch],
         compiler_params=params,
         name="advance",
-    )(returned.reshape(devices * half, entries), *prepared, walkers[0])
+    )(returned.reshape(devices * half, entries), *prepared, walkers[0], summand)
     return advanced[None], log_weight
 
 

time: 72.2 us -> 73.4 us (1.017)
  Pallas kernels: 21.5 us -> 22.7 us
    pallas_call x1, Pallas kernels: 7.53 us -> 10.4 us  [per_device(): pl.pallas_call(functools.partial(bias_kernel, walkers=devices, half=half,...]
    pallas_call x1, Pallas kernels: 1.21 us -> 0.05 us  [per_device(): pl.pallas_call(functools.partial(field_kernel, devices=devices), out_shap...]
where the time goes in v4:
time: 73.4 us; the launch traced here: 73.2 us
  blocking collectives  49.8 us (68%)
  Pallas kernels  22.7 us (31%)
    all_to_all x1, blocking collectives, per_device(): lax.all_to_all(outgoing.reshape(devices, half, entries), both, split_axis...  17.4 us
    all_to_all x1, blocking collectives, per_device(): lax.all_to_all(potential.reshape(devices, half, entries), both, split_axi...  12 us
    all_to_all x1, blocking collectives, per_device(): lax.all_to_all(partial_bias.reshape(devices, lanes, LANES), both, split_a...  10.6 us
    pallas_call x1, Pallas kernels, per_device(): pl.pallas_call(functools.partial(bias_kernel, walkers=devices, half=half,...  10.4 us
    all_to_all x1, blocking collectives, per_device(): fields = lax.all_to_all(fields, both, split_axis=0, concat_axis=0)  9.91 us
    pallas_call x1, Pallas kernels, per_device(): pl.pallas_call(functools.partial(potential_kernel, walkers=devices, nblk=...  6.39 us
    pallas_call x1, Pallas kernels, per_device(): pl.pallas_call(functools.partial(advance_kernel, side=side), out_shape=(j...  3.07 us
    pallas_call x1, Pallas kernels, per_device(): pl.pallas_call(functools.partial(green_kernel, **sizes), out_shape=jax.Sh...  2.79 us

profile of v4, /device:TPU:0, one launch (start us, length us, event | category | flops | bytes accessed | tf_op | source)
XLA Modules:
  0.0 73.2 jit_solution(445383067659782188)
XLA Ops:
  0.6 0.0 copy-start.1
  0.6 2.8 %green.1 = bf16[512,256]{1,0:T(8,128)(2,1)S(1)} custom-call(s32[16]{0:T(128)} %counts_hbm.3, s32[1,256]{1,0:T(1,128)} %bitcast.18, bf16[512,256]{1,0:T(8,128)(2,1)} %bitcast.20, bf16[512,256]{1,0:T(8,128)(2,1)} %trial_hbm.1), custom_call_target="tpu_custom_call" | custom-call | tf_op jit(solution)/shard_map/green/pallas_call | solution.py:331
  3.4 17.4 %all_to_all.20 = bf16[32,16,256]{2,1,0:T(8,128)(2,1)S(1)} all-to-all(bf16[32,16,256]{2,1,0:T(8,128)(2,1)S(1)} %bitcast.12), channel_id=1, replica_groups=mesh['groups'=2,'tile'=16] {'groups','tile'}, dimensions={0} | all-to-all | bytes 524288 | tf_op jit(solution)/shard_map/all_to_all | solution.py:349
  20.8 0.0 copy-start
  20.8 10.4 %bias.1 = (bf16[512,128]{1,0:T(8,128)(2,1)S(1)}, f32[16,128]{1,0:T(8,128)S(1)}, f32[16,128]{1,0:T(8,128)S(1)}) custom-call(bf16[512,256]{1,0:T(8,128)(2,1)S(1)} %bitcast.11, bf16[31,2048,256]{2,1,0:T(8,128)(2,1)} %chol_ref.3, s32[16,2048]{1,0:T(8,128)} %aux_hbm.1, s32[16,128]{1,0:T(8,128)} %bitcast.21, f32[4]{0:T(128)} %weight_hbm.1), custom_call_target="tpu_custom_call" | custom-call | flops 536870912 | bytes 16777216 | tf_op jit(solution)/shard_map/bias/pallas_call | solution.py:352
  31.2 10.6 %all_to_all.21.partial_ref = bf16[32,16,128]{2,1,0:T(8,128)(2,1)S(1)} all-to-all(bf16[32,16,128]{2,1,0:T(8,128)(2,1)S(1)} %bitcast.17), channel_id=1, replica_groups=mesh['groups'=2,'tile'=16] {'groups','tile'}, dimensions={0} | all-to-all | bytes 262144 | tf_op jit(solution)/shard_map/all_to_all | solution.py:384
  41.8 9.9 %all_to_all.22 = bf16[32,16,128]{2,1,0:T(8,128)(2,1)S(1)} all-to-all(bf16[32,16,128]{2,1,0:T(8,128)(2,1)S(1)} %get-tuple-element.17), channel_id=1, replica_groups=mesh['groups'=2,'tile'=16] {'groups','tile'}, dimensions={0} | all-to-all | bytes 262144 | tf_op jit(solution)/shard_map/all_to_all | solution.py:398
  51.7 0.0 copy-done.1
  51.7 6.4 %potential.1 = (bf16[512,256]{1,0:T(8,128)(2,1)S(1)}, bf16[256,512]{1,0:T(8,128)(2,1)S(1)}, bf16[256,2048]{1,0:T(8,128)(2,1)S(1)}, bf16[128,256]{1,0:T(8,128)(2,1)S(1)}, f32[256,128]{1,0:T(8,128)S(1)}) custom-call(s32[16]{0:T(128)} %counts_hbm.3, s32[1,256]{1,0:T(1,128)S(1)} %bitcast.19, bf16[512,128]{1,0:T(8,128)(2,1)S(1)} %bitcast.14, ...), custom_call_target="tpu_custom_call" | custom-call | flops 536870912 | bytes 16777216 | tf_op jit(solution)/shard_map/potential/pallas_call | solution.py:400
  58.1 12.0 %all_to_all.23 = bf16[32,16,256]{2,1,0:T(8,128)(2,1)S(1)} all-to-all(bf16[32,16,256]{2,1,0:T(8,128)(2,1)S(1)} %bitcast.15), channel_id=1, replica_groups=mesh['groups'=2,'tile'=16] {'groups','tile'}, dimensions={0} | all-to-all | bytes 524288 | tf_op jit(solution)/shard_map/all_to_all | solution.py:428
  70.1 0.0 copy-done
  70.1 3.1 %advance.1 = (bf16[512,256]{1,0:T(8,128)(2,1)}, f32[1]{0:T(128)}) custom-call(bf16[512,256]{1,0:T(8,128)(2,1)S(1)} %bitcast.13, bf16[256,512]{1,0:T(8,128)(2,1)S(1)} %get-tuple-element.19.place_ref, bf16[256,2048]{1,0:T(8,128)(2,1)S(1)} %get-tuple-element.20.spread_ref, bf16[128,256]{1,0:T(8,128)(2,1)S(1)} %get-tuple-element.21.pick_ref, ...), custom_call_target="tpu_custom_call" | custom-call | tf_op jit(solution)/shard_map/advance/pallas_call | solution.py:431
  (1 shorter events, 0.0 us)
Async XLA Ops:
  0.6 51.1 %copy-start.1 = (s32[256]{0:T(256)S(1)}, s32[256]{0:T(256)}, u32[]{:S(2)}) copy-start(s32[256]{0:T(256)} %param.13) | copy-start | bytes 3076
  20.8 49.3 %copy-start = (bf16[1,512,256]{2,1,0:T(8,128)(2,1)S(1)}, bf16[1,512,256]{2,1,0:T(8,128)(2,1)}, u32[]{:S(2)}) copy-start(bf16[1,512,256]{2,1,0:T(8,128)(2,1)} %param.9) | copy-start | bytes 786436

commit v5 on v3

--- a/solution.py
+++ b/solution.py
@@ -135,7 +135,9 @@
     return jnp.minimum(lax.axis_index("groups") * half, cap - half)
 
 
-def bias_kernel(green_ref, chol_ref, out_ref, tall, left, back, held, sems, *, walkers, half, block):
+def bias_kernel(
+    green_ref, chol_ref, out_ref, tall, left, back, held, sems, *, walkers, half, block
+):
     entries = green_ref.shape[1]
     vectors = held.shape[1]
     lanes = vectors // LANES
@@ -172,25 +174,23 @@
     out_ref[...] = back[...].astype(BF)
 
 
-def field_kernel(
-    weight_ref, partial_ref, aux_ref, group_ref, fields_ref, logw_ref, *, devices
-):
+def field_kernel(partial_ref, aux_ref, group_ref, weight_ref, fields_ref, summand_ref, *, devices):
     lanes = group_ref.shape[0]
-    bias = jnp.zeros((lanes, LANES), F32)
-    for i in range(devices):
+    bias = partial_ref[0].astype(F32)
+    for i in range(1, devices):
         bias = bias + partial_ref[i].astype(F32)
     draws = aux_ref[pl.ds(lax.axis_index("tile"), 1), :]
     draws = jnp.concatenate(
         [draws[:, i * LANES : (i + 1) * LANES] for i in range(lanes)], axis=0
     )
     sampled = draws.astype(F32) * (1.0 / 262144.0)
-    weight = jnp.zeros((lanes, LANES), F32)
-    for k in range(weight_ref.shape[0]):
-        weight = jnp.where(group_ref[...] == k, weight_ref[k], weight)
-    fields = (weight * (sampled - bias)).astype(BF)
+    scale = jnp.zeros((lanes, LANES), F32)
+    for k in range(weight_ref.shape[1]):
+        scale = jnp.where(group_ref[...] == k, weight_ref[:, k : k + 1], scale)
+    fields = (scale * (sampled - bias)).astype(BF)
     for i in range(devices):
         fields_ref[i] = fields
-    logw_ref[0] = jnp.sum(sampled * bias - 0.5 * bias * bias)
+    summand_ref[...] = sampled * bias - 0.5 * bias * bias
 
 
 def prepare(
@@ -212,9 +212,9 @@
 
 
 def potential_kernel(
-    counts_ref, pattern_ref, fields_ref, chol_ref,
+    counts_hbm, pattern_ref, fields_ref, chol_ref,
     out_ref, place_ref, spread_ref, pick_ref, inside_ref,
-    tall, left, back, held, sems, *, walkers, half, **sizes,
+    tall, left, back, held, counts_ref, counts_sem, sems, *, walkers, half, **sizes,
 ):
     entries = held.shape[2]
     lanes = left.shape[1] // LANES
@@ -228,7 +228,10 @@
         fetch(j).start()
         return carry
 
+    counts = pltpu.make_async_copy(counts_hbm, counts_ref, counts_sem)
+    counts.start()
     lax.fori_loop(0, half, begin, 0)
+    counts.wait()
     prepare(
         counts_ref, pattern_ref, place_ref, spread_ref, pick_ref, inside_ref, half=half, **sizes
     )
@@ -249,8 +252,10 @@
 
 
 def advance_kernel(
-    tiles_ref, place_ref, spread_ref, pick_ref, inside_ref, walker_ref, out_ref, wide_ref, *, side
-):
+    tiles_ref, place_ref, spread_ref, pick_ref, inside_ref, walker_ref, summand_ref,
+    out_ref, logw_ref, wide_ref, *, side,
+):
+    logw_ref[0] = jnp.sum(summand_ref[...])
     orbitals = walker_ref.shape[0]
     nblk = orbitals // side
     wide = orbitals // LANES
@@ -346,17 +351,17 @@
     partial_bias = lax.all_to_all(
         partial_bias.reshape(devices, lanes, LANES), both, split_axis=0, concat_axis=0
     )
-    fields, log_weight = pl.pallas_call(
+    fields, summand = pl.pallas_call(
         functools.partial(field_kernel, devices=devices),
         out_shape=(
             jax.ShapeDtypeStruct((devices, lanes, LANES), BF),
-            jax.ShapeDtypeStruct((1,), F32),
-        ),
-        in_specs=[smem, vmem, vmem, vmem],
-        out_specs=(vmem, smem),
+            jax.ShapeDtypeStruct((lanes, LANES), F32),
+        ),
+        in_specs=[vmem] * 4,
+        out_specs=(vmem,) * 2,
         compiler_params=params,
         name="fields",
-    )(group_weight, partial_bias, aux, chol_group.reshape(lanes, LANES))
+    )(partial_bias, aux, chol_group.reshape(lanes, LANES), group_weight.reshape(1, -1))
     fields = lax.all_to_all(fields, both, split_axis=0, concat_axis=0)
     spread_width = side * LANES
     potential, *prepared = pl.pallas_call(
@@ -370,13 +375,15 @@
             jax.ShapeDtypeStruct((LANES, tiles), BF),
             jax.ShapeDtypeStruct((tiles, LANES), F32),
         ),
-        in_specs=[smem, vmem, vmem, hbm],
+        in_specs=[in_hbm, vmem, vmem, hbm],
         out_specs=(vmem,) * 5,
         scratch_shapes=[
             pltpu.VMEM((devices * lanes, LANES), F32),
             pltpu.VMEM((devices, vectors), BF),
             pltpu.VMEM((entries // LANES, half * devices, LANES), F32),
             pltpu.VMEM((half, vectors, entries), BF),
+            pltpu.SMEM(owner_counts.shape, jnp.int32),
+            pltpu.SemaphoreType.DMA,
             pltpu.SemaphoreType.DMA((half,)),
         ],
         compiler_params=streaming,
@@ -384,19 +391,22 @@
             flops=flops, transcendentals=0, bytes_accessed=tile_bytes
         ),
         name="potential",
-    )(owner_counts, pattern_row, fields.reshape(devices * lanes, LANES), chol)
+    )(in_place(owner_counts), pattern_row, fields.reshape(devices * lanes, LANES), chol)
     returned = lax.all_to_all(
         potential.reshape(devices, half, entries), both, split_axis=0, concat_axis=0
     )
-    advanced = pl.pallas_call(
+    advanced, log_weight = pl.pallas_call(
         functools.partial(advance_kernel, side=side),
-        out_shape=jax.ShapeDtypeStruct((orbitals, electrons), BF),
-        in_specs=[vmem] * 6,
-        out_specs=vmem,
+        out_shape=(
+            jax.ShapeDtypeStruct((orbitals, electrons), BF),
+            jax.ShapeDtypeStruct((1,), F32),
+        ),
+        in_specs=[vmem] * 7,
+        out_specs=(vmem, smem),
         scratch_shapes=[wide_scratch],
         compiler_params=params,
         name="advance",
-    )(returned.reshape(devices * half, entries), *prepared, walkers[0])
+    )(returned.reshape(devices * half, entries), *prepared, walkers[0], summand)
     return advanced[None], log_weight
 
 

time: 72.2 us -> 70.7 us (0.979)
  Pallas kernels: 21.5 us -> 19.9 us
    pallas_call x1, Pallas kernels: 1.21 us -> 0.09 us  [per_device(): pl.pallas_call(functools.partial(field_kernel, devices=devices), out_shap...]
where the time goes in v5:
time: 70.7 us; the launch traced here: 70.5 us
  blocking collectives  49.8 us (70%)
  Pallas kernels  19.9 us (28%)
    all_to_all x1, blocking collectives, per_device(): lax.all_to_all(outgoing.reshape(devices, half, entries), both, split_axis...  17.4 us
    all_to_all x1, blocking collectives, per_device(): lax.all_to_all(potential.reshape(devices, half, entries), both, split_axi...  12 us
    all_to_all x1, blocking collectives, per_device(): lax.all_to_all(partial_bias.reshape(devices, lanes, LANES), both, split_a...  10.6 us
    all_to_all x1, blocking collectives, per_device(): fields = lax.all_to_all(fields, both, split_axis=0, concat_axis=0)  9.91 us
    pallas_call x1, Pallas kernels, per_device(): pl.pallas_call(functools.partial(bias_kernel, walkers=devices, half=half,...  7.53 us
    pallas_call x1, Pallas kernels, per_device(): pl.pallas_call(functools.partial(potential_kernel, walkers=devices, nblk=...  6.39 us
    pallas_call x1, Pallas kernels, per_device(): pl.pallas_call(functools.partial(advance_kernel, side=side), out_shape=(j...  3.07 us
    pallas_call x1, Pallas kernels, per_device(): pl.pallas_call(functools.partial(green_kernel, **sizes), out_shape=jax.Sh...  2.85 us

profile of v5, /device:TPU:0, one launch (start us, length us, event | category | flops | bytes accessed | tf_op | source)
XLA Modules:
  0.0 70.5 jit_solution(11559533069237619330)
XLA Ops:
  0.6 0.0 copy-start.3
  0.6 0.0 copy-start.1
  0.7 0.0 copy-start.4
  0.7 0.0 copy-start.2
  0.7 2.9 %green.1 = bf16[512,256]{1,0:T(8,128)(2,1)S(1)} custom-call(s32[16]{0:T(128)} %counts_hbm.3, s32[1,256]{1,0:T(1,128)} %bitcast.20, bf16[512,256]{1,0:T(8,128)(2,1)} %bitcast.23, bf16[512,256]{1,0:T(8,128)(2,1)} %trial_hbm.1), custom_call_target="tpu_custom_call" | custom-call | tf_op jit(solution)/shard_map/green/pallas_call | solution.py:312
  3.5 17.4 %all_to_all.20 = bf16[32,16,256]{2,1,0:T(8,128)(2,1)S(1)} all-to-all(bf16[32,16,256]{2,1,0:T(8,128)(2,1)S(1)} %bitcast.13), channel_id=1, replica_groups=mesh['groups'=2,'tile'=16] {'groups','tile'}, dimensions={0} | all-to-all | bytes 524288 | tf_op jit(solution)/shard_map/all_to_all | solution.py:330
  20.9 0.0 copy-start
  20.9 7.5 %bias.1 = bf16[512,128]{1,0:T(8,128)(2,1)S(1)} custom-call(bf16[512,256]{1,0:T(8,128)(2,1)S(1)} %bitcast.12, bf16[31,2048,256]{2,1,0:T(8,128)(2,1)} %chol_ref.3), custom_call_target="tpu_custom_call" | custom-call | flops 536870912 | bytes 16777216 | tf_op jit(solution)/shard_map/bias/pallas_call | solution.py:333
  28.5 10.6 %all_to_all.21.partial_ref = bf16[32,16,128]{2,1,0:T(8,128)(2,1)S(1)} all-to-all(bf16[32,16,128]{2,1,0:T(8,128)(2,1)S(1)} %bitcast.16), channel_id=1, replica_groups=mesh['groups'=2,'tile'=16] {'groups','tile'}, dimensions={0} | all-to-all | bytes 262144 | tf_op jit(solution)/shard_map/all_to_all | solution.py:351
  39.0 0.0 copy-done.1
  39.0 0.0 copy-done.4
  39.0 0.0 copy-done.2
  39.0 0.1 fields.1
  39.1 9.9 %all_to_all.22 = bf16[32,16,128]{2,1,0:T(8,128)(2,1)S(1)} all-to-all(bf16[32,16,128]{2,1,0:T(8,128)(2,1)S(1)} %get-tuple-element.11), channel_id=1, replica_groups=mesh['groups'=2,'tile'=16] {'groups','tile'}, dimensions={0} | all-to-all | bytes 262144 | tf_op jit(solution)/shard_map/all_to_all | solution.py:365
  49.0 0.0 copy-done.3
  49.0 6.4 %potential.1 = (bf16[512,256]{1,0:T(8,128)(2,1)S(1)}, bf16[256,512]{1,0:T(8,128)(2,1)S(1)}, bf16[256,2048]{1,0:T(8,128)(2,1)S(1)}, bf16[128,256]{1,0:T(8,128)(2,1)S(1)}, f32[256,128]{1,0:T(8,128)S(1)}) custom-call(s32[16]{0:T(128)} %counts_hbm.3, s32[1,256]{1,0:T(1,128)S(1)} %bitcast.21, bf16[512,128]{1,0:T(8,128)(2,1)S(1)} %bitcast.15, ...), custom_call_target="tpu_custom_call" | custom-call | flops 536870912 | bytes 16777216 | tf_op jit(solution)/shard_map/potential/pallas_call | solution.py:367
  55.4 12.0 %all_to_all.23 = bf16[32,16,256]{2,1,0:T(8,128)(2,1)S(1)} all-to-all(bf16[32,16,256]{2,1,0:T(8,128)(2,1)S(1)} %bitcast.17), channel_id=1, replica_groups=mesh['groups'=2,'tile'=16] {'groups','tile'}, dimensions={0} | all-to-all | bytes 524288 | tf_op jit(solution)/shard_map/all_to_all | solution.py:395
  67.4 0.0 copy-done
  67.4 3.1 %advance.1 = (bf16[512,256]{1,0:T(8,128)(2,1)}, f32[1]{0:T(128)}) custom-call(bf16[512,256]{1,0:T(8,128)(2,1)S(1)} %bitcast.14, bf16[256,512]{1,0:T(8,128)(2,1)S(1)} %get-tuple-element.13.place_ref, bf16[256,2048]{1,0:T(8,128)(2,1)S(1)} %get-tuple-element.14.spread_ref, bf16[128,256]{1,0:T(8,128)(2,1)S(1)} %get-tuple-element.15.pick_ref, ...), custom_call_target="tpu_custom_call" | custom-call | tf_op jit(solution)/shard_map/advance/pallas_call | solution.py:398
Async XLA Ops:
  0.6 48.4 %copy-start.3 = (s32[256]{0:T(256)S(1)}, s32[256]{0:T(256)}, u32[]{:S(2)}) copy-start(s32[256]{0:T(256)} %param.13) | copy-start | bytes 3076
  0.6 38.4 %copy-start.1 = (s32[16,2048]{1,0:T(8,128)S(1)}, s32[16,2048]{1,0:T(8,128)}, u32[]{:S(2)}) copy-start(s32[16,2048]{1,0:T(8,128)} %aux_ref.1) | copy-start | bytes 393220
  0.7 38.4 %copy-start.4 = (f32[4]{0:T(128)S(1)}, f32[4]{0:T(128)}, u32[]{:S(2)}) copy-start(f32[4]{0:T(128)} %param.16) | copy-start | bytes 52
  0.7 38.4 %copy-start.2 = (s32[2048]{0:T(1024)S(1)}, s32[2048]{0:T(1024)}, u32[]{:S(2)}) copy-start(s32[2048]{0:T(1024)} %param.15) | copy-start | bytes 24580
  20.9 46.5 %copy-start = (bf16[1,512,256]{2,1,0:T(8,128)(2,1)S(1)}, bf16[1,512,256]{2,1,0:T(8,128)(2,1)}, u32[]{:S(2)}) copy-start(bf16[1,512,256]{2,1,0:T(8,128)(2,1)} %param.9) | copy-start | bytes 786436

commit v6 on v5

--- a/solution.py
+++ b/solution.py
@@ -106,24 +106,33 @@
     green = nt(factor_ref[...], trial_ref[...])
     for k in range(wide):
         wide_ref[k] = green[:, k * LANES : (k + 1) * LANES]
-    cut = jnp.concatenate(
-        [
-            jnp.concatenate(
-                [wide_ref[k, pl.ds(p, nblk, stride=side), :] for p in range(side)], axis=1
-            ).astype(BF)
-            for k in range(wide)
-        ],
-        axis=0,
-    )
-    found = mm(pick, cut)
-    kept = jnp.concatenate(
-        [
-            jnp.where(inside, found[:, p * LANES : (p + 1) * LANES], 0.0).astype(BF)
-            for p in range(side)
-        ],
-        axis=1,
-    )
-    values = mm(kept, fold_ref[...]).astype(BF)
+    values = jnp.zeros((tiles, side * side), F32)
+    count = 2
+    for g in range(side // count):
+        cut = jnp.concatenate(
+            [
+                jnp.concatenate(
+                    [
+                        wide_ref[k, pl.ds(g * count + p, nblk, stride=side), :]
+                        for p in range(count)
+                    ],
+                    axis=1,
+                ).astype(BF)
+                for k in range(wide)
+            ],
+            axis=0,
+        )
+        found = mm(pick, cut)
+        kept = jnp.concatenate(
+            [
+                jnp.where(inside, found[:, p * LANES : (p + 1) * LANES], 0.0).astype(BF)
+                for p in range(count)
+            ],
+            axis=1,
+        )
+        span = count * LANES
+        values = values + mm(kept, fold_ref[g * span : (g + 1) * span, :])
+    values = values.astype(BF)
     out_ref[...] = mm(slot_ref[...], values).astype(BF)
 
 
@@ -273,10 +282,16 @@
                 k * nblk : (k + 1) * nblk, p * LANES : (p + 1) * LANES
             ]
     potential = jnp.concatenate([wide_ref[k].astype(BF) for k in range(wide)], axis=1)
-    term = walker_ref[...]
-    running = term.astype(F32)
+    terms = [walker_ref[...]]
+    rows = orbitals // 2
     for degree in range(1, 5):
-        term = (mm(potential, term) / degree).astype(BF)
+        term = [
+            (mm(potential[i * rows : (i + 1) * rows], terms[-1]) / degree).astype(BF)
+            for i in range(2)
+        ]
+        terms.append(jnp.concatenate(term, axis=0))
+    running = terms[0].astype(F32)
+    for term in terms[1:]:
         running = running + term.astype(F32)
     out_ref[...] = running.astype(BF)
 

time: 70.7 us -> 70.2 us (level)
  no operation moved by 1% of the time
where the time goes in v6:
time: 70.2 us; the launch traced here: 70 us
  blocking collectives  49.8 us (71%)
  Pallas kernels  19.5 us (28%)
    all_to_all x1, blocking collectives, per_device(): lax.all_to_all(outgoing.reshape(devices, half, entries), both, split_axis...  17.4 us
    all_to_all x1, blocking collectives, per_device(): lax.all_to_all(potential.reshape(devices, half, entries), both, split_axi...  12 us
    all_to_all x1, blocking collectives, per_device(): lax.all_to_all(partial_bias.reshape(devices, lanes, LANES), both, split_a...  10.6 us
    all_to_all x1, blocking collectives, per_device(): fields = lax.all_to_all(fields, both, split_axis=0, concat_axis=0)  9.91 us
    pallas_call x1, Pallas kernels, per_device(): pl.pallas_call(functools.partial(bias_kernel, walkers=devices, half=half,...  7.53 us
    pallas_call x1, Pallas kernels, per_device(): pl.pallas_call(functools.partial(potential_kernel, walkers=devices, nblk=...  6.39 us
    pallas_call x1, Pallas kernels, per_device(): pl.pallas_call(functools.partial(advance_kernel, side=side), out_shape=(j...  2.79 us
    pallas_call x1, Pallas kernels, per_device(): pl.pallas_call(functools.partial(green_kernel, **sizes), out_shape=jax.Sh...  2.69 us

profile of v6, /device:TPU:0, one launch (start us, length us, event | category | flops | bytes accessed | tf_op | source)
XLA Modules:
  0.0 70.0 jit_solution(3866398904214094163)
XLA Ops:
  0.6 0.0 copy-start.3
  0.6 0.0 copy-start.1
  0.7 0.0 copy-start.4
  0.7 0.0 copy-start.2
  0.7 2.7 %green.1 = bf16[512,256]{1,0:T(8,128)(2,1)S(1)} custom-call(s32[16]{0:T(128)} %counts_hbm.3, s32[1,256]{1,0:T(1,128)} %bitcast.20, bf16[512,256]{1,0:T(8,128)(2,1)} %bitcast.23, bf16[512,256]{1,0:T(8,128)(2,1)} %trial_hbm.1), custom_call_target="tpu_custom_call" | custom-call | tf_op jit(solution)/shard_map/green/pallas_call | solution.py:327
  3.4 17.4 %all_to_all.20 = bf16[32,16,256]{2,1,0:T(8,128)(2,1)S(1)} all-to-all(bf16[32,16,256]{2,1,0:T(8,128)(2,1)S(1)} %bitcast.13), channel_id=1, replica_groups=mesh['groups'=2,'tile'=16] {'groups','tile'}, dimensions={0} | all-to-all | bytes 524288 | tf_op jit(solution)/shard_map/all_to_all | solution.py:345
  20.8 0.0 copy-start
  20.8 7.5 %bias.1 = bf16[512,128]{1,0:T(8,128)(2,1)S(1)} custom-call(bf16[512,256]{1,0:T(8,128)(2,1)S(1)} %bitcast.12, bf16[31,2048,256]{2,1,0:T(8,128)(2,1)} %chol_ref.3), custom_call_target="tpu_custom_call" | custom-call | flops 536870912 | bytes 16777216 | tf_op jit(solution)/shard_map/bias/pallas_call | solution.py:348
  28.3 10.6 %all_to_all.21.partial_ref = bf16[32,16,128]{2,1,0:T(8,128)(2,1)S(1)} all-to-all(bf16[32,16,128]{2,1,0:T(8,128)(2,1)S(1)} %bitcast.16), channel_id=1, replica_groups=mesh['groups'=2,'tile'=16] {'groups','tile'}, dimensions={0} | all-to-all | bytes 262144 | tf_op jit(solution)/shard_map/all_to_all | solution.py:366
  38.8 0.0 copy-done.1
  38.8 0.0 copy-done.4
  38.8 0.0 copy-done.2
  38.8 0.1 fields.1
  38.9 9.9 %all_to_all.22 = bf16[32,16,128]{2,1,0:T(8,128)(2,1)S(1)} all-to-all(bf16[32,16,128]{2,1,0:T(8,128)(2,1)S(1)} %get-tuple-element.11), channel_id=1, replica_groups=mesh['groups'=2,'tile'=16] {'groups','tile'}, dimensions={0} | all-to-all | bytes 262144 | tf_op jit(solution)/shard_map/all_to_all | solution.py:380
  48.8 0.0 copy-done.3
  48.8 6.4 %potential.1 = (bf16[512,256]{1,0:T(8,128)(2,1)S(1)}, bf16[256,512]{1,0:T(8,128)(2,1)S(1)}, bf16[256,2048]{1,0:T(8,128)(2,1)S(1)}, bf16[128,256]{1,0:T(8,128)(2,1)S(1)}, f32[256,128]{1,0:T(8,128)S(1)}) custom-call(s32[16]{0:T(128)} %counts_hbm.3, s32[1,256]{1,0:T(1,128)S(1)} %bitcast.21, bf16[512,128]{1,0:T(8,128)(2,1)S(1)} %bitcast.15, ...), custom_call_target="tpu_custom_call" | custom-call | flops 536870912 | bytes 16777216 | tf_op jit(solution)/shard_map/potential/pallas_call | solution.py:382
  55.2 12.0 %all_to_all.23 = bf16[32,16,256]{2,1,0:T(8,128)(2,1)S(1)} all-to-all(bf16[32,16,256]{2,1,0:T(8,128)(2,1)S(1)} %bitcast.17), channel_id=1, replica_groups=mesh['groups'=2,'tile'=16] {'groups','tile'}, dimensions={0} | all-to-all | bytes 524288 | tf_op jit(solution)/shard_map/all_to_all | solution.py:410
  67.2 0.0 copy-done
  67.2 2.8 %advance.1 = (bf16[512,256]{1,0:T(8,128)(2,1)}, f32[1]{0:T(128)}) custom-call(bf16[512,256]{1,0:T(8,128)(2,1)S(1)} %bitcast.14, bf16[256,512]{1,0:T(8,128)(2,1)S(1)} %get-tuple-element.13.place_ref, bf16[256,2048]{1,0:T(8,128)(2,1)S(1)} %get-tuple-element.14.spread_ref, bf16[128,256]{1,0:T(8,128)(2,1)S(1)} %get-tuple-element.15.pick_ref, ...), custom_call_target="tpu_custom_call" | custom-call | tf_op jit(solution)/shard_map/advance/pallas_call | solution.py:413
Async XLA Ops:
  0.6 48.2 %copy-start.3 = (s32[256]{0:T(256)S(1)}, s32[256]{0:T(256)}, u32[]{:S(2)}) copy-start(s32[256]{0:T(256)} %param.13) | copy-start | bytes 3076
  0.6 38.2 %copy-start.1 = (s32[16,2048]{1,0:T(8,128)S(1)}, s32[16,2048]{1,0:T(8,128)}, u32[]{:S(2)}) copy-start(s32[16,2048]{1,0:T(8,128)} %aux_ref.1) | copy-start | bytes 393220
  0.7 38.2 %copy-start.4 = (f32[4]{0:T(128)S(1)}, f32[4]{0:T(128)}, u32[]{:S(2)}) copy-start(f32[4]{0:T(128)} %param.16) | copy-start | bytes 52
  0.7 38.2 %copy-start.2 = (s32[2048]{0:T(1024)S(1)}, s32[2048]{0:T(1024)}, u32[]{:S(2)}) copy-start(s32[2048]{0:T(1024)} %param.15) | copy-start | bytes 24580
  20.8 46.5 %copy-start = (bf16[1,512,256]{2,1,0:T(8,128)(2,1)S(1)}, bf16[1,512,256]{2,1,0:T(8,128)(2,1)}, u32[]{:S(2)}) copy-start(bf16[1,512,256]{2,1,0:T(8,128)(2,1)} %param.9) | copy-start | bytes 786436

commit v7 on v6

--- a/solution.py
+++ b/solution.py
@@ -34,6 +34,10 @@
 
 def nt(a, b):
     return lax.dot_general(a, b, (((1,), (1,)), ((), ())), preferred_element_type=F32)
+
+
+def tn(a, b):
+    return lax.dot_general(a, b, (((0,), (0,)), ((), ())), preferred_element_type=F32)
 
 
 def slot_of_tile(counts_ref, tiles, owners, groups, half, cap):
@@ -67,8 +71,9 @@
 
 
 def green_kernel(
-    counts_hbm, pattern_hbm, factor_hbm, trial_hbm, out_ref,
-    counts_ref, pattern_ref, factor_ref, trial_ref, wide_ref, fold_ref, slot_ref, sems,
+    counts_hbm, pattern_hbm, factor_hbm, trial_hbm,
+    out_ref, fold_ref, slot_ref, pick_ref, inside_ref,
+    counts_ref, pattern_ref, factor_ref, trial_ref, wide_ref, sems,
     *, owners, groups, half, cap, side,
 ):
     copies = [
@@ -99,6 +104,8 @@
     lane = iota((tiles, LANES), 1)
     pick = one_hot(where_row == lane)
     inside = place == (lane >> log2(side))
+    pick_ref[...] = pick
+    inside_ref[...] = jnp.where(inside, 1.0, 0.0)
     slot = slot_of_tile(counts_ref, tiles, owners, groups, half, cap)
     slot_ref[...] = one_hot(iota((slots, tiles), 0) == slot)
     copies[2].wait()
@@ -145,7 +152,7 @@
 
 
 def bias_kernel(
-    green_ref, chol_ref, out_ref, tall, left, back, held, sems, *, walkers, half, block
+    green_ref, chol_ref, out_ref, held, tall, left, back, sems, *, walkers, half, block
 ):
     entries = green_ref.shape[1]
     vectors = held.shape[1]
@@ -202,80 +209,44 @@
     summand_ref[...] = sampled * bias - 0.5 * bias * bias
 
 
-def prepare(
-    counts_ref, pattern_ref, place_ref, spread_ref, pick_ref, inside_ref, *, owners, groups, half, cap, side, nblk
-):
-    tiles, slots = place_ref.shape
-    lane = iota((tiles, LANES), 1)
-    slot = slot_of_tile(counts_ref, tiles, owners, groups, half, cap)
-    slot = jnp.broadcast_to(slot.astype(F32), (LANES, tiles)).T.astype(jnp.int32)
-    for k in range(slots // LANES):
-        place_ref[:, k * LANES : (k + 1) * LANES] = one_hot(slot == lane + k * LANES)
-    src = iota(spread_ref.shape, 0)
-    dst = iota(spread_ref.shape, 1)
-    spread_ref[...] = one_hot(((dst >> log2(LANES)) << log2(side)) + (dst & (side - 1)) == src)
-    where_row, _ = row_of(pattern_ref[...], nblk, side)
-    pick_ref[...] = one_hot(iota((LANES, tiles), 0) == where_row)
-    _, place = tile_columns(pattern_ref, tiles, nblk, side)
-    inside_ref[...] = jnp.where(place == (lane >> log2(side)), 1.0, 0.0)
-
-
-def potential_kernel(
-    counts_hbm, pattern_ref, fields_ref, chol_ref,
-    out_ref, place_ref, spread_ref, pick_ref, inside_ref,
-    tall, left, back, held, counts_ref, counts_sem, sems, *, walkers, half, **sizes,
-):
+def potential_kernel(fields_ref, held, out_ref, tall, left, back, *, walkers, half):
     entries = held.shape[2]
     lanes = left.shape[1] // LANES
     narrow = entries // LANES
-    first = first_slot(half, chol_ref.shape[0])
-
-    def fetch(j):
-        return pltpu.make_async_copy(chol_ref.at[first + j], held.at[j], sems.at[j])
-
-    def begin(j, carry):
-        fetch(j).start()
-        return carry
-
-    counts = pltpu.make_async_copy(counts_hbm, counts_ref, counts_sem)
-    counts.start()
-    lax.fori_loop(0, half, begin, 0)
-    counts.wait()
-    prepare(
-        counts_ref, pattern_ref, place_ref, spread_ref, pick_ref, inside_ref, half=half, **sizes
-    )
     tall[...] = fields_ref[...].astype(F32)
     for i in range(lanes):
         left[:, i * LANES : (i + 1) * LANES] = tall[pl.ds(i, walkers, stride=lanes), :].astype(BF)
-
-    def step(j, carry):
-        fetch(j).wait()
-        tile = mm(left[...], held[j])
-        for k in range(narrow):
-            back[k, pl.ds(j, walkers, stride=half), :] = tile[:, k * LANES : (k + 1) * LANES]
+    count = 4 if half % 4 == 0 else 1
+
+    def step(s, carry):
+        for i in range(count):
+            j = s * count + i
+            tile = mm(left[...], held[j])
+            for k in range(narrow):
+                back[k, pl.ds(j, walkers, stride=half), :] = tile[:, k * LANES : (k + 1) * LANES]
         return carry
 
-    lax.fori_loop(0, half, step, 0)
+    lax.fori_loop(0, half // count, step, 0)
     for k in range(narrow):
         out_ref[:, k * LANES : (k + 1) * LANES] = back[k].astype(BF)
 
 
 def advance_kernel(
-    tiles_ref, place_ref, spread_ref, pick_ref, inside_ref, walker_ref, summand_ref,
+    tiles_ref, fold_ref, slot_ref, pick_ref, inside_ref, walker_ref, summand_ref,
     out_ref, logw_ref, wide_ref, *, side,
 ):
     logw_ref[0] = jnp.sum(summand_ref[...])
     orbitals = walker_ref.shape[0]
     nblk = orbitals // side
     wide = orbitals // LANES
-    values = mm(place_ref[...], tiles_ref[...]).astype(BF)
-    repeated = mm(values, spread_ref[...])
+    values = tn(slot_ref[...], tiles_ref[...]).astype(BF)
+    repeated = nt(values, fold_ref[...])
     inside = inside_ref[...]
     kept = jnp.concatenate(
         [(repeated[:, p * LANES : (p + 1) * LANES] * inside).astype(BF) for p in range(side)],
         axis=1,
     )
-    cut = mm(pick_ref[...], kept)
+    cut = tn(pick_ref[...], kept)
     for k in range(wide):
         for p in range(side):
             wide_ref[k, pl.ds(p, nblk, stride=side), :] = cut[
@@ -324,19 +295,23 @@
     flops = 2 * devices * half * vectors * entries
     wide_scratch = pltpu.VMEM((orbitals // LANES, orbitals, LANES), F32)
 
-    outgoing = pl.pallas_call(
+    outgoing, *choices = pl.pallas_call(
         functools.partial(green_kernel, **sizes),
-        out_shape=jax.ShapeDtypeStruct((devices * half, entries), BF),
+        out_shape=(
+            jax.ShapeDtypeStruct((devices * half, entries), BF),
+            jax.ShapeDtypeStruct((side * LANES, entries), BF),
+            jax.ShapeDtypeStruct((devices * half, tiles), BF),
+            jax.ShapeDtypeStruct((tiles, LANES), BF),
+            jax.ShapeDtypeStruct((tiles, LANES), F32),
+        ),
         in_specs=[in_hbm] * 4,
-        out_specs=vmem,
+        out_specs=(vmem,) * 5,
         scratch_shapes=[
             pltpu.SMEM(owner_counts.shape, jnp.int32),
             pltpu.VMEM((1, tiles), jnp.int32),
             pltpu.VMEM((orbitals, electrons), BF),
             pltpu.VMEM((orbitals, electrons), BF),
             wide_scratch,
-            pltpu.VMEM((side * LANES, entries), BF),
-            pltpu.VMEM((devices * half, tiles), BF),
             pltpu.SemaphoreType.DMA((4,)),
         ],
         compiler_params=params,
@@ -345,16 +320,18 @@
     arrived = lax.all_to_all(
         outgoing.reshape(devices, half, entries), both, split_axis=0, concat_axis=0
     )
-    partial_bias = pl.pallas_call(
+    partial_bias, held = pl.pallas_call(
         functools.partial(bias_kernel, walkers=devices, half=half, block=block),
-        out_shape=jax.ShapeDtypeStruct((devices * lanes, LANES), BF),
+        out_shape=(
+            jax.ShapeDtypeStruct((devices * lanes, LANES), BF),
+            jax.ShapeDtypeStruct((half, vectors, entries), BF),
+        ),
         in_specs=[vmem, hbm],
-        out_specs=vmem,
+        out_specs=(vmem,) * 2,
         scratch_shapes=[
             pltpu.VMEM((entries // LANES, half * devices, LANES), F32),
             pltpu.VMEM((devices, half * entries), BF),
             pltpu.VMEM((devices * lanes, LANES), F32),
-            pltpu.VMEM((half, vectors, entries), BF),
             pltpu.SemaphoreType.DMA((vectors // block,)),
         ],
         compiler_params=streaming,
@@ -378,35 +355,22 @@
         name="fields",
     )(partial_bias, aux, chol_group.reshape(lanes, LANES), group_weight.reshape(1, -1))
     fields = lax.all_to_all(fields, both, split_axis=0, concat_axis=0)
-    spread_width = side * LANES
-    potential, *prepared = pl.pallas_call(
-        functools.partial(
-            potential_kernel, walkers=devices, nblk=orbitals // side, **sizes
-        ),
-        out_shape=(
-            jax.ShapeDtypeStruct((devices * half, entries), BF),
-            jax.ShapeDtypeStruct((tiles, devices * half), BF),
-            jax.ShapeDtypeStruct((entries, spread_width), BF),
-            jax.ShapeDtypeStruct((LANES, tiles), BF),
-            jax.ShapeDtypeStruct((tiles, LANES), F32),
-        ),
-        in_specs=[in_hbm, vmem, vmem, hbm],
-        out_specs=(vmem,) * 5,
+    potential = pl.pallas_call(
+        functools.partial(potential_kernel, walkers=devices, half=half),
+        out_shape=jax.ShapeDtypeStruct((devices * half, entries), BF),
+        in_specs=[vmem, vmem],
+        out_specs=vmem,
         scratch_shapes=[
             pltpu.VMEM((devices * lanes, LANES), F32),
             pltpu.VMEM((devices, vectors), BF),
             pltpu.VMEM((entries // LANES, half * devices, LANES), F32),
-            pltpu.VMEM((half, vectors, entries), BF),
-            pltpu.SMEM(owner_counts.shape, jnp.int32),
-            pltpu.SemaphoreType.DMA,
-            pltpu.SemaphoreType.DMA((half,)),
         ],
         compiler_params=streaming,
         cost_estimate=pl.CostEstimate(
             flops=flops, transcendentals=0, bytes_accessed=tile_bytes
         ),
         name="potential",
-    )(in_place(owner_counts), pattern_row, fields.reshape(devices * lanes, LANES), chol)
+    )(fields.reshape(devices * lanes, LANES), held)
     returned = lax.all_to_all(
         potential.reshape(devices, half, entries), both, split_axis=0, concat_axis=0
     )
@@ -421,7 +385,7 @@
         scratch_shapes=[wide_scratch],
         compiler_params=params,
         name="advance",
-    )(returned.reshape(devices * half, entries), *prepared, walkers[0], summand)
+    )(returned.reshape(devices * half, entries), *choices, walkers[0], summand)
     return advanced[None], log_weight
 
 

time: 70.2 us -> 67.3 us (0.959)
  Pallas kernels: 19.5 us -> 16.5 us
    pallas_call x2, Pallas kernels: 9.08 us -> 6.14 us  [the longest x1 3.5 us: per_device(): pl.pallas_call(functools.partial(potential_kernel, walkers=devices, half=...]
where the time goes in v7:
time: 67.3 us; the launch traced here: 67 us
  blocking collectives  49.8 us (74%)
  Pallas kernels  16.5 us (25%)
  between operations  0.7 us (1%)
    all_to_all x1, blocking collectives, per_device(): lax.all_to_all(outgoing.reshape(devices, half, entries), both, split_axis...  17.4 us
    all_to_all x1, blocking collectives, per_device(): lax.all_to_all(potential.reshape(devices, half, entries), both, split_axi...  12 us
    all_to_all x1, blocking collectives, per_device(): lax.all_to_all(partial_bias.reshape(devices, lanes, LANES), both, split_a...  10.6 us
    all_to_all x1, blocking collectives, per_device(): fields = lax.all_to_all(fields, both, split_axis=0, concat_axis=0)  9.91 us
    pallas_call x1, Pallas kernels, per_device(): pl.pallas_call(functools.partial(bias_kernel, walkers=devices, half=half,...  7.49 us
    pallas_call x1, Pallas kernels, per_device(): pl.pallas_call(functools.partial(potential_kernel, walkers=devices, half=...  3.5 us
    pallas_call x1, Pallas kernels, per_device(): pl.pallas_call(functools.partial(advance_kernel, side=side), out_shape=(j...  2.81 us
    pallas_call x1, Pallas kernels, per_device(): pl.pallas_call(functools.partial(green_kernel, **sizes), out_shape=(jax.S...  2.63 us

profile of v7, /device:TPU:0, one launch (start us, length us, event | category | flops | bytes accessed | tf_op | source)
XLA Modules:
  0.0 67.0 jit_solution(10510842930200608478)
XLA Ops:
  0.6 0.0 copy-start.1
  0.6 0.0 copy-start.3
  0.7 0.0 copy-start.2
  0.7 0.0 copy-start
  0.7 2.6 %green.1 = (bf16[512,256]{1,0:T(8,128)(2,1)S(1)}, bf16[2048,256]{1,0:T(8,128)(2,1)S(1)}, bf16[512,256]{1,0:T(8,128)(2,1)S(1)}, bf16[256,128]{1,0:T(8,128)(2,1)S(1)}, f32[256,128]{1,0:T(8,128)S(1)}) custom-call(s32[16]{0:T(128)} %counts_hbm.1, s32[1,256]{1,0:T(1,128)} %bitcast.22, bf16[512,256]{1,0:T(8,128)(2,1)} %bitcast.21, bf16[512,256]{1,0:T(8,128)(2,1)} %trial_hbm.1), custom_call_target="tpu_custom_call" | custom-call | tf_op jit(solution)/shard_map/green/pallas_call | solution.py:298
  3.3 17.4 %all_to_all.20 = bf16[32,16,256]{2,1,0:T(8,128)(2,1)S(1)} all-to-all(bf16[32,16,256]{2,1,0:T(8,128)(2,1)S(1)} %bitcast.16), channel_id=1, replica_groups=mesh['groups'=2,'tile'=16] {'groups','tile'}, dimensions={0} | all-to-all | bytes 524288 | tf_op jit(solution)/shard_map/all_to_all | solution.py:320
  20.7 7.5 %bias.1 = (bf16[512,128]{1,0:T(8,128)(2,1)S(1)}, bf16[16,2048,256]{2,1,0:T(8,128)(2,1)S(1)}) custom-call(bf16[512,256]{1,0:T(8,128)(2,1)S(1)} %bitcast.12, bf16[31,2048,256]{2,1,0:T(8,128)(2,1)} %chol_ref.1), custom_call_target="tpu_custom_call" | custom-call | flops 536870912 | bytes 16777216 | tf_op jit(solution)/shard_map/bias/pallas_call | solution.py:323
  28.2 10.6 %all_to_all.21.partial_ref = bf16[32,16,128]{2,1,0:T(8,128)(2,1)S(1)} all-to-all(bf16[32,16,128]{2,1,0:T(8,128)(2,1)S(1)} %bitcast.18), channel_id=1, replica_groups=mesh['groups'=2,'tile'=16] {'groups','tile'}, dimensions={0} | all-to-all | bytes 262144 | tf_op jit(solution)/shard_map/all_to_all | solution.py:343
  38.7 0.0 copy-done.1
  38.7 0.0 copy-done.3
  38.8 0.0 copy-done.2
  38.8 0.1 fields.1
  38.8 9.9 %all_to_all.22 = bf16[32,16,128]{2,1,0:T(8,128)(2,1)S(1)} all-to-all(bf16[32,16,128]{2,1,0:T(8,128)(2,1)S(1)} %get-tuple-element.15), channel_id=1, replica_groups=mesh['groups'=2,'tile'=16] {'groups','tile'}, dimensions={0} | all-to-all | bytes 262144 | tf_op jit(solution)/shard_map/all_to_all | solution.py:357
  48.8 3.5 %potential.1 = bf16[512,256]{1,0:T(8,128)(2,1)S(1)} custom-call(bf16[512,128]{1,0:T(8,128)(2,1)S(1)} %bitcast.15, bf16[16,2048,256]{2,1,0:T(8,128)(2,1)S(1)} %get-tuple-element.16.held), custom_call_target="tpu_custom_call" | custom-call | flops 536870912 | bytes 16777216 | tf_op jit(solution)/shard_map/potential/pallas_call | solution.py:358
  52.3 12.0 %all_to_all.23 = bf16[32,16,256]{2,1,0:T(8,128)(2,1)S(1)} all-to-all(bf16[32,16,256]{2,1,0:T(8,128)(2,1)S(1)} %bitcast.13), channel_id=1, replica_groups=mesh['groups'=2,'tile'=16] {'groups','tile'}, dimensions={0} | all-to-all | bytes 524288 | tf_op jit(solution)/shard_map/all_to_all | solution.py:374
  64.2 0.0 copy-done
  64.2 2.8 %advance.1 = (bf16[512,256]{1,0:T(8,128)(2,1)}, f32[1]{0:T(128)}) custom-call(bf16[512,256]{1,0:T(8,128)(2,1)S(1)} %bitcast.14, bf16[2048,256]{1,0:T(8,128)(2,1)S(1)} %get-tuple-element.17.fold_ref, bf16[512,256]{1,0:T(8,128)(2,1)S(1)} %get-tuple-element.18.slot_ref, bf16[256,128]{1,0:T(8,128)(2,1)S(1)} %get-tuple-element.19.pick_ref, ...), custom_call_target="tpu_custom_call" | custom-call | tf_op jit(solution)/shard_map/advance/pallas_call | solution.py:377
Async XLA Ops:
  0.6 38.1 %copy-start.1 = (s32[16,2048]{1,0:T(8,128)S(1)}, s32[16,2048]{1,0:T(8,128)}, u32[]{:S(2)}) copy-start(s32[16,2048]{1,0:T(8,128)} %aux_ref.1) | copy-start | bytes 393220
  0.6 38.1 %copy-start.3 = (f32[4]{0:T(128)S(1)}, f32[4]{0:T(128)}, u32[]{:S(2)}) copy-start(f32[4]{0:T(128)} %param.16) | copy-start | bytes 52
  0.7 38.1 %copy-start.2 = (s32[2048]{0:T(1024)S(1)}, s32[2048]{0:T(1024)}, u32[]{:S(2)}) copy-start(s32[2048]{0:T(1024)} %param.15) | copy-start | bytes 24580
  0.7 63.6 %copy-start = (bf16[1,512,256]{2,1,0:T(8,128)(2,1)S(1)}, bf16[1,512,256]{2,1,0:T(8,128)(2,1)}, u32[]{:S(2)}) copy-start(bf16[1,512,256]{2,1,0:T(8,128)(2,1)} %param.9) | copy-start | bytes 786436

commit v8 on v7

--- a/solution.py
+++ b/solution.py
@@ -71,8 +71,8 @@
 
 
 def green_kernel(
-    counts_hbm, pattern_hbm, factor_hbm, trial_hbm,
-    out_ref, fold_ref, slot_ref, pick_ref, inside_ref,
+    counts_hbm, pattern_hbm, factor_hbm, trial_hbm, chol_ref,
+    out_ref, fold_ref, slot_ref, pick_ref, inside_ref, early_ref,
     counts_ref, pattern_ref, factor_ref, trial_ref, wide_ref, sems,
     *, owners, groups, half, cap, side,
 ):
@@ -110,6 +110,12 @@
     slot_ref[...] = one_hot(iota((slots, tiles), 0) == slot)
     copies[2].wait()
     copies[3].wait()
+    early = pltpu.make_async_copy(
+        chol_ref.at[pl.ds(first_slot(half, cap), half), pl.ds(0, early_ref.shape[1]), :],
+        early_ref,
+        sems.at[4],
+    )
+    early.start()
     green = nt(factor_ref[...], trial_ref[...])
     for k in range(wide):
         wide_ref[k] = green[:, k * LANES : (k + 1) * LANES]
@@ -141,6 +147,7 @@
         values = values + mm(kept, fold_ref[g * span : (g + 1) * span, :])
     values = values.astype(BF)
     out_ref[...] = mm(slot_ref[...], values).astype(BF)
+    early.wait()
 
 
 def in_place(x):
@@ -152,19 +159,22 @@
 
 
 def bias_kernel(
-    green_ref, chol_ref, out_ref, held, tall, left, back, sems, *, walkers, half, block
+    green_ref, early_ref, chol_ref, out_ref, held, tall, left, back, sems,
+    *, walkers, half, block,
 ):
     entries = green_ref.shape[1]
-    vectors = held.shape[1]
-    lanes = vectors // LANES
+    ready = early_ref.shape[1]
+    lanes = (ready + held.shape[1]) // LANES
     narrow = entries // LANES
-    steps = vectors // block
+    steps = held.shape[1] // block
     first = first_slot(half, chol_ref.shape[0])
 
     def fetch(s):
         rows = pl.ds(s * block if isinstance(s, int) else pl.multiple_of(s * block, block), block)
+        start = ready + s * block
+        source = pl.ds(start if isinstance(s, int) else pl.multiple_of(start, block), block)
         return pltpu.make_async_copy(
-            chol_ref.at[pl.ds(first, half), rows, :], held.at[:, rows, :], sems.at[s]
+            chol_ref.at[pl.ds(first, half), source, :], held.at[:, rows, :], sems.at[s]
         )
 
     for s in range(steps):
@@ -176,16 +186,24 @@
             at = j * entries + k * LANES
             left[:, at : at + LANES] = tall[k, pl.ds(j, walkers, stride=half), :].astype(BF)
 
+    def product(source, s, base):
+        rows = pl.ds(pl.multiple_of(s * block, block), block)
+        right = jnp.concatenate([source[j, rows, :] for j in range(half)], axis=1)
+        total = nt(left[...], right)
+        for i in range(block // LANES):
+            place = base + s * (block // LANES) + i
+            back[pl.ds(place, walkers, stride=lanes), :] = total[:, i * LANES : (i + 1) * LANES]
+
+    def first_step(s, carry):
+        product(early_ref, s, 0)
+        return carry
+
     def step(s, carry):
         fetch(s).wait()
-        rows = pl.ds(pl.multiple_of(s * block, block), block)
-        right = jnp.concatenate([held[j, rows, :] for j in range(half)], axis=1)
-        total = nt(left[...], right)
-        for i in range(block // LANES):
-            place = s * (block // LANES) + i
-            back[pl.ds(place, walkers, stride=lanes), :] = total[:, i * LANES : (i + 1) * LANES]
+        product(held, s, ready // LANES)
         return carry
 
+    lax.fori_loop(0, ready // block, first_step, 0)
     lax.fori_loop(0, steps, step, 0)
     out_ref[...] = back[...].astype(BF)
 
@@ -209,7 +227,10 @@
     summand_ref[...] = sampled * bias - 0.5 * bias * bias
 
 
-def potential_kernel(fields_ref, held, out_ref, tall, left, back, *, walkers, half):
+def potential_kernel(
+    fields_ref, early_ref, held, out_ref, tall, left, back, *, walkers, half
+):
+    ready = early_ref.shape[1]
     entries = held.shape[2]
     lanes = left.shape[1] // LANES
     narrow = entries // LANES
@@ -221,7 +242,7 @@
     def step(s, carry):
         for i in range(count):
             j = s * count + i
-            tile = mm(left[...], held[j])
+            tile = mm(left[:, :ready], early_ref[j]) + mm(left[:, ready:], held[j])
             for k in range(narrow):
                 back[k, pl.ds(j, walkers, stride=half), :] = tile[:, k * LANES : (k + 1) * LANES]
         return carry
@@ -284,18 +305,18 @@
     smem = pl.BlockSpec(memory_space=pltpu.SMEM)
     vmem = pl.BlockSpec(memory_space=pltpu.VMEM)
     params = pltpu.CompilerParams(vmem_limit_bytes=VMEM_LIMIT)
-    hbm = pl.BlockSpec(memory_space=pl.ANY)
     in_hbm = pl.BlockSpec(memory_space=pltpu.HBM)
     streaming = pltpu.CompilerParams(
         vmem_limit_bytes=VMEM_LIMIT + 2 * half * vectors * entries
     )
     sizes = dict(owners=owners, groups=groups, half=half, cap=cap, side=side)
-    block = min(256, vectors)
+    block = min(256, vectors // 2)
+    ready = block
     tile_bytes = half * vectors * entries * 2
     flops = 2 * devices * half * vectors * entries
     wide_scratch = pltpu.VMEM((orbitals // LANES, orbitals, LANES), F32)
 
-    outgoing, *choices = pl.pallas_call(
+    outgoing, *choices, early = pl.pallas_call(
         functools.partial(green_kernel, **sizes),
         out_shape=(
             jax.ShapeDtypeStruct((devices * half, entries), BF),
@@ -303,20 +324,21 @@
             jax.ShapeDtypeStruct((devices * half, tiles), BF),
             jax.ShapeDtypeStruct((tiles, LANES), BF),
             jax.ShapeDtypeStruct((tiles, LANES), F32),
-        ),
-        in_specs=[in_hbm] * 4,
-        out_specs=(vmem,) * 5,
+            jax.ShapeDtypeStruct((half, ready, entries), BF),
+        ),
+        in_specs=[in_hbm] * 5,
+        out_specs=(vmem,) * 6,
         scratch_shapes=[
             pltpu.SMEM(owner_counts.shape, jnp.int32),
             pltpu.VMEM((1, tiles), jnp.int32),
             pltpu.VMEM((orbitals, electrons), BF),
             pltpu.VMEM((orbitals, electrons), BF),
             wide_scratch,
-            pltpu.SemaphoreType.DMA((4,)),
+            pltpu.SemaphoreType.DMA((5,)),
         ],
         compiler_params=params,
         name="green",
-    )(*(in_place(x) for x in (owner_counts, pattern_row, green_factor[0], trial)))
+    )(*(in_place(x) for x in (owner_counts, pattern_row, green_factor[0], trial)), in_place(chol))
     arrived = lax.all_to_all(
         outgoing.reshape(devices, half, entries), both, split_axis=0, concat_axis=0
     )
@@ -324,22 +346,22 @@
         functools.partial(bias_kernel, walkers=devices, half=half, block=block),
         out_shape=(
             jax.ShapeDtypeStruct((devices * lanes, LANES), BF),
-            jax.ShapeDtypeStruct((half, vectors, entries), BF),
-        ),
-        in_specs=[vmem, hbm],
+            jax.ShapeDtypeStruct((half, vectors - ready, entries), BF),
+        ),
+        in_specs=[vmem, vmem, in_hbm],
         out_specs=(vmem,) * 2,
         scratch_shapes=[
             pltpu.VMEM((entries // LANES, half * devices, LANES), F32),
             pltpu.VMEM((devices, half * entries), BF),
             pltpu.VMEM((devices * lanes, LANES), F32),
-            pltpu.SemaphoreType.DMA((vectors // block,)),
+            pltpu.SemaphoreType.DMA(((vectors - ready) // block,)),
         ],
         compiler_params=streaming,
         cost_estimate=pl.CostEstimate(
             flops=flops, transcendentals=0, bytes_accessed=tile_bytes
         ),
         name="bias",
-    )(arrived.reshape(devices * half, entries), chol)
+    )(arrived.reshape(devices * half, entries), early, in_place(chol))
     partial_bias = lax.all_to_all(
         partial_bias.reshape(devices, lanes, LANES), both, split_axis=0, concat_axis=0
     )
@@ -358,7 +380,7 @@
     potential = pl.pallas_call(
         functools.partial(potential_kernel, walkers=devices, half=half),
         out_shape=jax.ShapeDtypeStruct((devices * half, entries), BF),
-        in_specs=[vmem, vmem],
+        in_specs=[vmem] * 3,
         out_specs=vmem,
         scratch_shapes=[
             pltpu.VMEM((devices * lanes, LANES), F32),
@@ -370,7 +392,7 @@
             flops=flops, transcendentals=0, bytes_accessed=tile_bytes
         ),
         name="potential",
-    )(fields.reshape(devices * lanes, LANES), held)
+    )(fields.reshape(devices * lanes, LANES), early, held)
     returned = lax.all_to_all(
         potential.reshape(devices, half, entries), both, split_axis=0, concat_axis=0
     )

time: 67.3 us -> 68.5 us (1.018)
  Pallas kernels: 16.5 us -> 17.7 us
    pallas_call x1, Pallas kernels: 2.63 us -> 3.97 us  [per_device(): pl.pallas_call(functools.partial(green_kernel, **sizes), out_shape=(jax.S...]
where the time goes in v8:
time: 68.5 us; the launch traced here: 68.2 us
  blocking collectives  49.8 us (73%)
  Pallas kernels  17.7 us (26%)
    all_to_all x1, blocking collectives, per_device(): lax.all_to_all(outgoing.reshape(devices, half, entries), both, split_axis...  17.4 us
    all_to_all x1, blocking collectives, per_device(): lax.all_to_all(potential.reshape(devices, half, entries), both, split_axi...  12 us
    all_to_all x1, blocking collectives, per_device(): lax.all_to_all(partial_bias.reshape(devices, lanes, LANES), both, split_a...  10.6 us
    all_to_all x1, blocking collectives, per_device(): fields = lax.all_to_all(fields, both, split_axis=0, concat_axis=0)  9.91 us
    pallas_call x1, Pallas kernels, per_device(): pl.pallas_call(functools.partial(bias_kernel, walkers=devices, half=half,...  7.37 us
    pallas_call x1, Pallas kernels, per_device(): pl.pallas_call(functools.partial(green_kernel, **sizes), out_shape=(jax.S...  3.97 us
    pallas_call x1, Pallas kernels, per_device(): pl.pallas_call(functools.partial(potential_kernel, walkers=devices, half=...  3.52 us
    pallas_call x1, Pallas kernels, per_device(): pl.pallas_call(functools.partial(advance_kernel, side=side), out_shape=(j...  2.81 us

profile of v8, /device:TPU:0, one launch (start us, length us, event | category | flops | bytes accessed | tf_op | source)
XLA Modules:
  0.0 68.2 jit_solution(2670262615580111348)
XLA Ops:
  0.6 4.0 %green.1 = (bf16[512,256]{1,0:T(8,128)(2,1)S(1)}, bf16[2048,256]{1,0:T(8,128)(2,1)S(1)}, bf16[512,256]{1,0:T(8,128)(2,1)S(1)}, bf16[256,128]{1,0:T(8,128)(2,1)S(...) custom-call(s32[16]{0:T(128)} %counts_hbm.1, s32[1,256]{1,0:T(1,128)} %bitcast.22, ...), custom_call_target="tpu_custom_call" | custom-call | tf_op jit(solution)/shard_map/green/pallas_call | solution.py:319
  4.6 17.4 %all_to_all.20 = bf16[32,16,256]{2,1,0:T(8,128)(2,1)S(1)} all-to-all(bf16[32,16,256]{2,1,0:T(8,128)(2,1)S(1)} %bitcast.16), channel_id=1, replica_groups=mesh['groups'=2,'tile'=16] {'groups','tile'}, dimensions={0} | all-to-all | bytes 524288 | tf_op jit(solution)/shard_map/all_to_all | solution.py:342
  22.0 0.0 copy-start.1
  22.0 0.0 copy-start.2
  22.0 0.0 copy-start.3
  22.0 7.4 %bias.1 = (bf16[512,128]{1,0:T(8,128)(2,1)S(1)}, bf16[16,1792,256]{2,1,0:T(8,128)(2,1)S(1)}) custom-call(bf16[512,256]{1,0:T(8,128)(2,1)S(1)} %bitcast.12, bf16[16,256,256]{2,1,0:T(8,128)(2,1)S(1)} %get-tuple-element.15.early_ref, bf16[31,2048,256]{2,1,0:T(8,128)(2,1)} %chol_ref.3), custom_call_target="tpu_custom_call" | custom-call | flops 536870912 | bytes 16777216 | tf_op jit(solution)/shard_map/bias/pallas_call | solution.py:345
  29.4 0.0 copy-start
  29.4 10.6 %all_to_all.21.partial_ref = bf16[32,16,128]{2,1,0:T(8,128)(2,1)S(1)} all-to-all(bf16[32,16,128]{2,1,0:T(8,128)(2,1)S(1)} %bitcast.18), channel_id=1, replica_groups=mesh['groups'=2,'tile'=16] {'groups','tile'}, dimensions={0} | all-to-all | bytes 262144 | tf_op jit(solution)/shard_map/all_to_all | solution.py:365
  39.9 0.0 copy-done.1
  39.9 0.0 copy-done.2
  39.9 0.0 copy-done.3
  39.9 0.1 fields.1
  40.0 9.9 %all_to_all.22 = bf16[32,16,128]{2,1,0:T(8,128)(2,1)S(1)} all-to-all(bf16[32,16,128]{2,1,0:T(8,128)(2,1)S(1)} %get-tuple-element.17), channel_id=1, replica_groups=mesh['groups'=2,'tile'=16] {'groups','tile'}, dimensions={0} | all-to-all | bytes 262144 | tf_op jit(solution)/shard_map/all_to_all | solution.py:379
  49.9 3.5 %potential.1 = bf16[512,256]{1,0:T(8,128)(2,1)S(1)} custom-call(bf16[512,128]{1,0:T(8,128)(2,1)S(1)} %bitcast.15, bf16[16,256,256]{2,1,0:T(8,128)(2,1)S(1)} %get-tuple-element.15.early_ref, bf16[16,1792,256]{2,1,0:T(8,128)(2,1)S(1)} %get-tuple-element.18.held), custom_call_target="tpu_custom_call" | custom-call | flops 536870912 | bytes 16777216 | tf_op jit(solution)/shard_map/potential/pallas_call | solution.py:380
  53.5 12.0 %all_to_all.23 = bf16[32,16,256]{2,1,0:T(8,128)(2,1)S(1)} all-to-all(bf16[32,16,256]{2,1,0:T(8,128)(2,1)S(1)} %bitcast.13), channel_id=1, replica_groups=mesh['groups'=2,'tile'=16] {'groups','tile'}, dimensions={0} | all-to-all | bytes 524288 | tf_op jit(solution)/shard_map/all_to_all | solution.py:396
  65.4 0.0 copy-done
  65.4 2.8 %advance.1 = (bf16[512,256]{1,0:T(8,128)(2,1)}, f32[1]{0:T(128)}) custom-call(bf16[512,256]{1,0:T(8,128)(2,1)S(1)} %bitcast.14, bf16[2048,256]{1,0:T(8,128)(2,1)S(1)} %get-tuple-element.19.fold_ref, bf16[512,256]{1,0:T(8,128)(2,1)S(1)} %get-tuple-element.20.slot_ref, bf16[256,128]{1,0:T(8,128)(2,1)S(1)} %get-tuple-element.21.pick_ref, ...), custom_call_target="tpu_custom_call" | custom-call | tf_op jit(solution)/shard_map/advance/pallas_call | solution.py:399
Async XLA Ops:
  22.0 17.9 %copy-start.1 = (s32[16,2048]{1,0:T(8,128)S(1)}, s32[16,2048]{1,0:T(8,128)}, u32[]{:S(2)}) copy-start(s32[16,2048]{1,0:T(8,128)} %aux_ref.1) | copy-start | bytes 393220
  22.0 17.9 %copy-start.2 = (s32[2048]{0:T(1024)S(1)}, s32[2048]{0:T(1024)}, u32[]{:S(2)}) copy-start(s32[2048]{0:T(1024)} %param.15) | copy-start | bytes 24580
  22.0 17.9 %copy-start.3 = (f32[4]{0:T(128)S(1)}, f32[4]{0:T(128)}, u32[]{:S(2)}) copy-start(f32[4]{0:T(128)} %param.16) | copy-start | bytes 52
  29.4 36.1 %copy-start = (bf16[1,512,256]{2,1,0:T(8,128)(2,1)S(1)}, bf16[1,512,256]{2,1,0:T(8,128)(2,1)}, u32[]{:S(2)}) copy-start(bf16[1,512,256]{2,1,0:T(8,128)(2,1)} %param.9) | copy-start | bytes 786436

commit v9 on v7

--- a/solution.py
+++ b/solution.py
@@ -216,7 +216,7 @@
     tall[...] = fields_ref[...].astype(F32)
     for i in range(lanes):
         left[:, i * LANES : (i + 1) * LANES] = tall[pl.ds(i, walkers, stride=lanes), :].astype(BF)
-    count = 4 if half % 4 == 0 else 1
+    count = 8 if half % 8 == 0 else 1
 
     def step(s, carry):
         for i in range(count):

time: 67.3 us -> 67 us (level)
  no operation moved by 1% of the time
where the time goes in v9:
time: 67 us; the launch traced here: 66.8 us
  blocking collectives  49.8 us (74%)
  Pallas kernels  16.3 us (24%)
  between operations  0.7 us (1%)
    all_to_all x1, blocking collectives, per_device(): lax.all_to_all(outgoing.reshape(devices, half, entries), both, split_axis...  17.4 us
    all_to_all x1, blocking collectives, per_device(): lax.all_to_all(potential.reshape(devices, half, entries), both, split_axi...  12 us
    all_to_all x1, blocking collectives, per_device(): lax.all_to_all(partial_bias.reshape(devices, lanes, LANES), both, split_a...  10.6 us
    all_to_all x1, blocking collectives, per_device(): fields = lax.all_to_all(fields, both, split_axis=0, concat_axis=0)  9.91 us
    pallas_call x1, Pallas kernels, per_device(): pl.pallas_call(functools.partial(bias_kernel, walkers=devices, half=half,...  7.49 us
    pallas_call x1, Pallas kernels, per_device(): pl.pallas_call(functools.partial(potential_kernel, walkers=devices, half=...  3.26 us
    pallas_call x1, Pallas kernels, per_device(): pl.pallas_call(functools.partial(advance_kernel, side=side), out_shape=(j...  2.81 us
    pallas_call x1, Pallas kernels, per_device(): pl.pallas_call(functools.partial(green_kernel, **sizes), out_shape=(jax.S...  2.63 us

profile of v9, /device:TPU:0, one launch (start us, length us, event | category | flops | bytes accessed | tf_op | source)
XLA Modules:
  0.0 66.8 jit_solution(11191900749377180210)
XLA Ops:
  0.6 0.0 copy-start.1
  0.6 0.0 copy-start.3
  0.7 0.0 copy-start.2
  0.7 0.0 copy-start
  0.7 2.6 %green.1 = (bf16[512,256]{1,0:T(8,128)(2,1)S(1)}, bf16[2048,256]{1,0:T(8,128)(2,1)S(1)}, bf16[512,256]{1,0:T(8,128)(2,1)S(1)}, bf16[256,128]{1,0:T(8,128)(2,1)S(1)}, f32[256,128]{1,0:T(8,128)S(1)}) custom-call(s32[16]{0:T(128)} %counts_hbm.1, s32[1,256]{1,0:T(1,128)} %bitcast.22, bf16[512,256]{1,0:T(8,128)(2,1)} %bitcast.21, bf16[512,256]{1,0:T(8,128)(2,1)} %trial_hbm.1), custom_call_target="tpu_custom_call" | custom-call | tf_op jit(solution)/shard_map/green/pallas_call | solution.py:298
  3.3 17.4 %all_to_all.20 = bf16[32,16,256]{2,1,0:T(8,128)(2,1)S(1)} all-to-all(bf16[32,16,256]{2,1,0:T(8,128)(2,1)S(1)} %bitcast.16), channel_id=1, replica_groups=mesh['groups'=2,'tile'=16] {'groups','tile'}, dimensions={0} | all-to-all | bytes 524288 | tf_op jit(solution)/shard_map/all_to_all | solution.py:320
  20.7 7.5 %bias.1 = (bf16[512,128]{1,0:T(8,128)(2,1)S(1)}, bf16[16,2048,256]{2,1,0:T(8,128)(2,1)S(1)}) custom-call(bf16[512,256]{1,0:T(8,128)(2,1)S(1)} %bitcast.12, bf16[31,2048,256]{2,1,0:T(8,128)(2,1)} %chol_ref.1), custom_call_target="tpu_custom_call" | custom-call | flops 536870912 | bytes 16777216 | tf_op jit(solution)/shard_map/bias/pallas_call | solution.py:323
  28.2 10.6 %all_to_all.21.partial_ref = bf16[32,16,128]{2,1,0:T(8,128)(2,1)S(1)} all-to-all(bf16[32,16,128]{2,1,0:T(8,128)(2,1)S(1)} %bitcast.18), channel_id=1, replica_groups=mesh['groups'=2,'tile'=16] {'groups','tile'}, dimensions={0} | all-to-all | bytes 262144 | tf_op jit(solution)/shard_map/all_to_all | solution.py:343
  38.7 0.0 copy-done.1
  38.7 0.0 copy-done.3
  38.8 0.0 copy-done.2
  38.8 0.1 fields.1
  38.8 9.9 %all_to_all.22 = bf16[32,16,128]{2,1,0:T(8,128)(2,1)S(1)} all-to-all(bf16[32,16,128]{2,1,0:T(8,128)(2,1)S(1)} %get-tuple-element.15), channel_id=1, replica_groups=mesh['groups'=2,'tile'=16] {'groups','tile'}, dimensions={0} | all-to-all | bytes 262144 | tf_op jit(solution)/shard_map/all_to_all | solution.py:357
  48.8 3.3 %potential.1 = bf16[512,256]{1,0:T(8,128)(2,1)S(1)} custom-call(bf16[512,128]{1,0:T(8,128)(2,1)S(1)} %bitcast.15, bf16[16,2048,256]{2,1,0:T(8,128)(2,1)S(1)} %get-tuple-element.16.held), custom_call_target="tpu_custom_call" | custom-call | flops 536870912 | bytes 16777216 | tf_op jit(solution)/shard_map/potential/pallas_call | solution.py:358
  52.0 12.0 %all_to_all.23 = bf16[32,16,256]{2,1,0:T(8,128)(2,1)S(1)} all-to-all(bf16[32,16,256]{2,1,0:T(8,128)(2,1)S(1)} %bitcast.13), channel_id=1, replica_groups=mesh['groups'=2,'tile'=16] {'groups','tile'}, dimensions={0} | all-to-all | bytes 524288 | tf_op jit(solution)/shard_map/all_to_all | solution.py:374
  64.0 0.0 copy-done
  64.0 2.8 %advance.1 = (bf16[512,256]{1,0:T(8,128)(2,1)}, f32[1]{0:T(128)}) custom-call(bf16[512,256]{1,0:T(8,128)(2,1)S(1)} %bitcast.14, bf16[2048,256]{1,0:T(8,128)(2,1)S(1)} %get-tuple-element.17.fold_ref, bf16[512,256]{1,0:T(8,128)(2,1)S(1)} %get-tuple-element.18.slot_ref, bf16[256,128]{1,0:T(8,128)(2,1)S(1)} %get-tuple-element.19.pick_ref, ...), custom_call_target="tpu_custom_call" | custom-call | tf_op jit(solution)/shard_map/advance/pallas_call | solution.py:377
Async XLA Ops:
  0.6 38.1 %copy-start.1 = (s32[16,2048]{1,0:T(8,128)S(1)}, s32[16,2048]{1,0:T(8,128)}, u32[]{:S(2)}) copy-start(s32[16,2048]{1,0:T(8,128)} %aux_ref.1) | copy-start | bytes 393220
  0.6 38.1 %copy-start.3 = (f32[4]{0:T(128)S(1)}, f32[4]{0:T(128)}, u32[]{:S(2)}) copy-start(f32[4]{0:T(128)} %param.16) | copy-start | bytes 52
  0.7 38.1 %copy-start.2 = (s32[2048]{0:T(1024)S(1)}, s32[2048]{0:T(1024)}, u32[]{:S(2)}) copy-start(s32[2048]{0:T(1024)} %param.15) | copy-start | bytes 24580
  0.7 63.3 %copy-start = (bf16[1,512,256]{2,1,0:T(8,128)(2,1)S(1)}, bf16[1,512,256]{2,1,0:T(8,128)(2,1)}, u32[]{:S(2)}) copy-start(bf16[1,512,256]{2,1,0:T(8,128)(2,1)} %param.9) | copy-start | bytes 786436
